TPU v7x, 32 devices: a whole 2x2x4 slice. The times are simulated.
32 devices in a mesh: level: 2 (over core), dom: 8 (over z, x), samp: 2 (over y).
Axes of the slice: x: 2, y: 2, z: 4, core: 2. Of those that a mesh axis runs over, the one named last changes fastest.
Arguments:
- panels: float32 [2, 4096, 16, 256], P('level', 'dom', None, 'samp'), may hold values from 0 to 2
- courant: float32 [4096, 4, 256], P('dom', None, 'samp'), may hold values from 0.3 to 0.95
- direction: int32 [4096, 4, 2], P('dom', None, 'samp'), may hold values 0 or 1
- decay: float32 [4096], P('dom'), may hold values from 0.02 to 0.8
- booster: float32 [4096], P('dom'), may hold values from 0 to 1
- feeder: int32 [4096, 2], P('dom'), may hold values from 0 to 767, as said below
- face_index: int32 [1024], P('dom'), may hold values from 0 to 511
Outputs:
- advanced: float32 [2, 4096, 16, 256], P('level', 'dom', None, 'samp')
- level_gap: float32 [4096, 4, 256], P('dom', 'level', 'samp')
Inputs may be any that keep to these rules, and one draw needn't show every extreme that they name: `feeder`: entries below 512 name the partition's own pipes, the next 128 name the face pipes of the partition before it, the last 128 those of the partition after it. Most entries are below 512. `face_index`: local pipe numbers within the partition; repeats may occur.
All inputs are finite; a program needn't handle non-finite values. No bound on the sum of `direction` on one device may be relied on, other than what follows from the above.
Results may differ from a plain program's by a relative error of at most 0.00016.
Values sent between devices are 32-bit elements; how exact they have to be, the bound alone decides.
No kernel may reach another device: no remote copies, remote signals or barrier semaphores. Data moves between devices by JAX's collectives and lax.ppermute only.
A program may use at most 128 MiB of HBM per device.

v0:
```python
import jax
import jax.numpy as jnp
from jax import lax
from jax.experimental import pallas as pl
from jax.experimental.pallas import tpu as pltpu
from jax.sharding import PartitionSpec as P

SEGF = 16
SEGC = 4
GROUPS = SEGF // SEGC
LANES = 128
CHUNKS = 8

HBM = pl.BlockSpec(memory_space=pltpu.HBM)
VMEM = pl.BlockSpec(memory_space=pltpu.VMEM)
SMEM = pl.BlockSpec(memory_space=pltpu.SMEM)


def params():
    return pltpu.CompilerParams(vmem_limit_bytes=8 << 20)


def cost(nbytes):
    return pl.CostEstimate(flops=0, bytes_accessed=nbytes, transcendentals=0)


def pinned(space, *arrays):
    return [pltpu.with_memory_space_constraint(x, space) for x in arrays]


def down_rows(row):
    return jnp.broadcast_to(row, (LANES, LANES)).T


def spread(ref, row):
    return ref[pl.ds(row, 8, stride=0), :]


def load_kernel(
    panel, rate, dirs, feed, decay, boost, faces,
    cells, rates, outflow, factor, boosts, table, face_rows,
    flow_back, dir_v, feed_v, decay_v, boost_v, face_s, panel_sem, rate_sem, small_sem,
):
    rows = panel.shape[0] // CHUNKS
    blocks = decay.shape[0]
    pipes = blocks * LANES
    level = lax.axis_index("level")

    def chunk(n):
        part = pl.ds(pl.multiple_of(n * rows, rows), rows)
        return pltpu.make_async_copy(panel.at[part], cells.at[part], panel_sem.at[n])

    small = [
        pltpu.make_async_copy(src, dst, small_sem.at[n])
        for n, (src, dst) in enumerate(
            ((dirs, dir_v), (decay, decay_v), (feed, feed_v), (boost, boost_v), (faces, face_s))
        )
    ]
    rate_copy = pltpu.make_async_copy(rate, rates, rate_sem)
    for copy in small:
        copy.start()
    rate_copy.start()
    for n in range(CHUNKS):
        chunk(n).start()
    for copy in small:
        copy.wait()

    scale = jnp.where(level == 0, jnp.float32(-0.25), jnp.float32(-1.0))
    fac = jnp.exp(decay_v[...] * scale)
    for b in range(blocks):
        own = slice(b * LANES, (b + 1) * LANES)
        factor[own, :] = down_rows(fac[b : b + 1])
        boosts[own, :] = down_rows(boost_v[b : b + 1])
    outflow[GROUPS * pipes :, :] = jnp.zeros_like(outflow[GROUPS * pipes :, :])
    back = (dir_v[...] == 1).astype(jnp.int32)
    for b in range(blocks):
        ahead = feed_v[2 * b : 2 * b + 1, :]
        behind = feed_v[2 * b + 1 : 2 * b + 2, :]
        revs, ghost = [], []
        for g in range(GROUPS):
            at = g * blocks + b
            rev = back[at : at + 1, :]
            src = jnp.where(rev == 1, behind, ahead)
            table[at : at + 1, :] = src * GROUPS + g
            revs.append(rev)
            ghost.append((src >= pipes).astype(jnp.int32))
        for t in range(2):
            at = (GROUPS + t) * blocks + b
            table[at : at + 1, :] = 8 * (revs[2 * t] + 2 * revs[2 * t + 1])
        at = (GROUPS + 2) * blocks + b
        every = jnp.maximum(jnp.maximum(ghost[0], ghost[1]), jnp.maximum(ghost[2], ghost[3]))
        table[at : at + 1, :] = jnp.where(level == 0, ghost[0], every)

    backf = back.astype(jnp.float32)

    def back_rows(g):
        for b in range(blocks):
            at = g * blocks + b
            flow_back[at * LANES : (at + 1) * LANES, :] = down_rows(backf[at : at + 1])

    back_rows(0)

    @pl.when(level == 1)
    def _():
        for g in range(1, GROUPS):
            back_rows(g)

    rate_copy.wait()
    per_chunk = pipes // 8 // CHUNKS

    @pl.when(level == 0)
    def _():
        @pl.loop(0, CHUNKS)
        def _(n):
            chunk(n).wait()
            for i in range(per_chunk):
                q = n * per_chunk + i
                base = pl.multiple_of(q * 128, 128)
                own = pl.ds(pl.multiple_of(q * 8, 8), 8)
                rev = flow_back[own, :] != 0.0
                b = factor[own, :] * rates[pl.ds(pl.multiple_of(q * 32, 32), 8, stride=4), :]
                a = factor[own, :] - b
                y = [
                    jnp.where(
                        rev,
                        cells[pl.ds(base + j, 8, stride=16), :],
                        cells[pl.ds(base + 15 - j, 8, stride=16), :],
                    )
                    for j in range(GROUPS)
                ]
                for s in range(GROUPS):
                    outflow[pl.ds(pl.multiple_of(q * 32, 32) + s, 8, stride=4), :] = y[0]
                    y = [a * y[j] + b * y[j + 1] for j in range(len(y) - 1)]

    @pl.when(level == 1)
    def _():
        @pl.loop(0, CHUNKS)
        def _(n):
            chunk(n).wait()
            for i in range(per_chunk):
                q = n * per_chunk + i
                base = pl.multiple_of(q * 128, 128)
                for g in range(GROUPS):
                    rev = flow_back[pl.ds(pl.multiple_of(g * pipes + q * 8, 8), 8), :] != 0.0
                    outflow[pl.ds(pl.multiple_of(q * 32, 32) + g, 8, stride=4), :] = jnp.where(
                        rev,
                        cells[pl.ds(base + 4 * g, 8, stride=16), :],
                        cells[pl.ds(base + 4 * g + 3, 8, stride=16), :],
                    )

    @pl.loop(0, faces.shape[0] // 8)
    def _(m):
        for u in range(8):
            pipe = face_s[m * 8 + u]
            face_rows[pl.ds(pl.multiple_of(m * 32, 32) + 4 * u, 4), :] = outflow[
                pl.ds(pl.multiple_of(pipe * 4, 4), 4), :
            ]


def fine_pipe(p, rev, src, cells, rates, outflow, factor, boosts, new):
    near = pl.ds(pl.multiple_of(p * 16 + 8 * rev, 8), 8)
    far = pl.ds(pl.multiple_of(p * 16 + 8 - 8 * rev, 8), 8)
    f = spread(factor, p)
    b = f * spread(rates, p * 4)
    a = f - b
    bo = spread(boosts, p)
    y0, y1 = cells[near, :], cells[far, :]
    shift = 1 + 6 * rev
    edge = lax.broadcasted_iota(jnp.int32, (8, LANES), 0) == 7 * rev
    for s in range(GROUPS):
        inflow = spread(outflow, src + s) + bo
        q0 = pltpu.roll(y0, shift, 0)
        q1 = pltpu.roll(y1, shift, 0)
        y1 = a * y1 + b * jnp.where(edge, q0, q1)
        y0 = a * y0 + b * jnp.where(edge, inflow, q0)
    new[near, :] = y0
    new[far, :] = y1


def coarse_pipe(p, srcs, codes, masks, cells, rates, outflow, factor, boosts, new):
    low = lax.broadcasted_iota(jnp.int32, (8, LANES), 0) < 4
    f = spread(factor, p)
    bo = spread(boosts, p)
    for t in range(2):
        own = pl.ds(pl.multiple_of(p * 16 + 8 * t, 8), 8)
        x = cells[own, :]
        r = jnp.where(low, spread(rates, p * 4 + 2 * t), spread(rates, p * 4 + 2 * t + 1))
        inflow = jnp.where(low, spread(outflow, srcs[2 * t]), spread(outflow, srcs[2 * t + 1])) + bo
        code = pl.multiple_of(codes[t], 8)
        turned = masks[pl.ds(code, 8), :] != 0.0
        edge = masks[pl.ds(32 + code, 8), :] != 0.0
        up = jnp.where(edge, inflow, jnp.where(turned, pltpu.roll(x, 7, 0), pltpu.roll(x, 1, 0)))
        b = f * r
        new[own, :] = (f - b) * x + b * up


def fill_masks(masks):
    row = lax.broadcasted_iota(jnp.int32, (8, LANES), 0)
    for code in range(4):
        rev = jnp.where(row < 4, code & 1, code >> 1)
        masks[8 * code : 8 * code + 8, :] = rev.astype(jnp.float32)
        edge = (row & 3) == 3 * rev
        masks[32 + 8 * code : 40 + 8 * code, :] = edge.astype(jnp.float32)


def one_pipe(fine, p, b, j, table, dirs, masks, *state):
    blocks = dirs.shape[0] // GROUPS
    if fine:
        fine_pipe(p, dirs[b, j], table[b, j], *state)
    else:
        srcs = [table[g * blocks + b, j] for g in range(GROUPS)]
        codes = [table[(GROUPS + t) * blocks + b, j] for t in range(2)]
        coarse_pipe(p, srcs, codes, masks, *state)


def step_kernel(
    table, dirs, cells, rates, outflow, factor, boosts,
    new, out, keep, send, ghosts,
    masks, sems,
):
    blocks = dirs.shape[0] // GROUPS
    level = lax.axis_index("level")
    fill_masks(masks)

    def written(b):
        part = pl.ds(pl.multiple_of(b * 16 * LANES, 128), 16 * LANES)
        return pltpu.make_async_copy(new.at[part], out.at[part], sems.at[b])

    def run(fine):
        def block(b, count):
            def some(m, count):
                for u in range(8):
                    j = m * 8 + u
                    p = b * LANES + j
                    one_pipe(
                        fine, p, b, j, table, dirs, masks,
                        cells, rates, outflow, factor, boosts, new,
                    )
                    ghosts[count] = p
                    count = count + table[(GROUPS + 2) * blocks + b, j]
                return count

            count = lax.fori_loop(0, LANES // 8, some, count)
            written(b).start()

            @pl.loop(0, LANES // 8)
            def _(m):
                q = b * (LANES // 8) + m
                base = pl.multiple_of(q * 128, 128)
                for k in range(SEGC):
                    if fine:
                        part = [new[pl.ds(base + 4 * k + i, 8, stride=16), :] for i in range(4)]
                        share = ((part[0] + part[1]) + (part[2] + part[3])) * 0.25
                    else:
                        share = new[pl.ds(base + k, 8, stride=16), :]
                    dest = keep if (k < 2) == fine else send
                    dest[pl.ds(pl.multiple_of(q * 16, 16) + k % 2, 8, stride=2), :] = share

            return count

        count = lax.fori_loop(0, blocks, block, jnp.int32(0))
        last = ghosts[jnp.maximum(count - 1, 0)]
        for u in range(8):
            ghosts[count + u] = last
        ghosts[blocks * LANES + 8] = count

    @pl.when(level == 0)
    def _():
        run(True)

    @pl.when(level == 1)
    def _():
        run(False)

    for b in range(blocks):
        written(b).wait()


def arrive_kernel(first, rows, near, arrived, outflow_in, outflow):
    odd = lax.axis_index("dom") % 2
    half = arrived.shape[0]
    slot = 1 - odd if near else odd
    start = pl.multiple_of(first + slot * half, 8)
    outflow[pl.ds(start, half), :] = arrived[...]


def fix_kernel(
    first, table, dirs, ghosts, arrived, cells, rates, factor, boosts,
    outflow_in, new_in, keep_in, send_in,
    outflow, new, keep, send,
    masks,
):
    blocks = dirs.shape[0] // GROUPS
    level = lax.axis_index("level")
    arrive_kernel(first, 0, False, arrived, outflow_in, outflow)
    fill_masks(masks)
    count = ghosts[blocks * LANES + 8]

    def run(fine):
        @pl.loop(0, (count + 3) // 4)
        def _(m):
            pipes = [ghosts[m * 4 + u] for u in range(4)]
            for p in pipes:
                one_pipe(
                    fine, p, p // LANES, p % LANES, table, dirs, masks,
                    cells, rates, outflow, factor, boosts, new,
                )
            for p in pipes:
                if fine:
                    part = [new[pl.ds(p * 16 + i, 4, stride=4), :] for i in range(4)]
                    share = ((part[0] + part[1]) + (part[2] + part[3])) * 0.25
                else:
                    share = new[pl.ds(pl.multiple_of(p * 16, 16), 4), :]
                own = pl.ds(p * 2, 2)
                keep[own, :] = share[0:2] if fine else share[2:4]
                send[own, :] = share[2:4] if fine else share[0:2]

    @pl.when(level == 0)
    def _():
        run(True)

    @pl.when(level == 1)
    def _():
        run(False)


def gap_kernel(keep, partner, gap):
    sign = jnp.where(lax.axis_index("level") == 0, jnp.float32(1.0), jnp.float32(-1.0))
    gap[...] = (keep[...] - partner[...]) * sign


def write_kernel(ghosts, new, out_in, out, sems):
    pipes = new.shape[0] // SEGF
    count = ghosts[pipes + 8]

    def moved(i):
        part = pl.ds(pl.multiple_of(ghosts[i] * 16, 16), 16)
        return pltpu.make_async_copy(new.at[part], out.at[part], sems.at[i])

    @pl.loop(0, count)
    def _(i):
        moved(i).start()

    @pl.loop(0, count)
    def _(i):
        moved(i).wait()


def per_device(panels, courant, direction, decay, booster, feeder, face_index):
    pipes = panels.shape[1]
    columns = panels.shape[3]
    faces = face_index.shape[0]
    blocks = pipes // LANES
    domains = lax.axis_size("dom")
    f32, i32 = jnp.float32, jnp.int32
    cells_in = panels.reshape(pipes * SEGF, columns)
    rates_in = courant.reshape(pipes * GROUPS, columns)
    dirs = direction.transpose(1, 2, 0).reshape(GROUPS * blocks, LANES)
    feed = feeder.reshape(blocks, LANES, 2).transpose(0, 2, 1).reshape(2 * blocks, LANES)
    ghost_rows = GROUPS * (pipes + 2 * faces)

    cells, rates, outflow, factor, boosts, table, face_rows = pl.pallas_call(
        load_kernel,
        name="load_step",
        in_specs=[HBM] * 7,
        out_specs=[VMEM] * 7,
        out_shape=[
            pltpu.VMEM((pipes * SEGF, columns), f32),
            pltpu.VMEM((pipes * GROUPS, columns), f32),
            pltpu.VMEM((ghost_rows, columns), f32),
            pltpu.VMEM((pipes, columns), f32),
            pltpu.VMEM((pipes, columns), f32),
            jax.ShapeDtypeStruct(((GROUPS + 4) * blocks, LANES), i32),
            pltpu.VMEM((faces * GROUPS, columns), f32),
        ],
        scratch_shapes=[
            pltpu.VMEM((GROUPS * pipes, columns), f32),
            pltpu.VMEM(dirs.shape, i32),
            pltpu.VMEM(feed.shape, i32),
            pltpu.VMEM((blocks, LANES), f32),
            pltpu.VMEM((blocks, LANES), f32),
            pltpu.SMEM((faces,), i32),
            pltpu.SemaphoreType.DMA((CHUNKS,)),
            pltpu.SemaphoreType.DMA(()),
            pltpu.SemaphoreType.DMA((5,)),
        ],
        compiler_params=params(),
        cost_estimate=cost(5 << 20),
    )(
        *pinned(
            pltpu.HBM, cells_in, rates_in, dirs, feed,
            decay.reshape(blocks, LANES), booster.reshape(blocks, LANES), face_index,
        )
    )

    near_pairs = [(i, i ^ 1) for i in range(domains) if i ^ 1 < domains]
    far_pairs = [(i, i + 1) for i in range(1, domains - 1, 2)]
    far_pairs = far_pairs + [(j, i) for i, j in far_pairs]
    near_rows = lax.ppermute(face_rows, "dom", near_pairs)
    far_rows = lax.ppermute(face_rows, "dom", far_pairs)

    new, out, keep, send, ghosts = pl.pallas_call(
        step_kernel,
        name="advance_step",
        in_specs=[SMEM] * 2 + [VMEM] * 5,
        out_specs=[VMEM, HBM, VMEM, VMEM, SMEM],
        out_shape=[
            pltpu.VMEM((pipes * SEGF, columns), f32),
            jax.ShapeDtypeStruct((pipes * SEGF, columns), f32),
            pltpu.VMEM((pipes * 2, columns), f32),
            pltpu.VMEM((pipes * 2, columns), f32),
            jax.ShapeDtypeStruct((pipes + 16,), i32),
        ],
        scratch_shapes=[pltpu.VMEM((64, columns), f32), pltpu.SemaphoreType.DMA((blocks,))],
        compiler_params=params(),
        cost_estimate=cost(20 << 20),
    )(table, dirs, cells, rates, outflow, factor, boosts)

    first = GROUPS * pipes
    outflow = pl.pallas_call(
        lambda *refs: arrive_kernel(first, 0, True, *refs),
        name="near_arrive",
        in_specs=[VMEM] * 2,
        out_specs=VMEM,
        out_shape=pltpu.VMEM((ghost_rows, columns), f32),
        input_output_aliases={1: 0},
        compiler_params=params(),
        cost_estimate=cost(1 << 19),
    )(near_rows, outflow)

    outflow, new, keep, send = pl.pallas_call(
        lambda *refs: fix_kernel(first, *refs),
        name="ghost_fix",
        in_specs=[SMEM] * 3 + [VMEM] * 9,
        out_specs=[VMEM] * 4,
        out_shape=[
            pltpu.VMEM((ghost_rows, columns), f32),
            pltpu.VMEM((pipes * SEGF, columns), f32),
            pltpu.VMEM((pipes * 2, columns), f32),
            pltpu.VMEM((pipes * 2, columns), f32),
        ],
        scratch_shapes=[pltpu.VMEM((64, columns), f32)],
        input_output_aliases={8: 0, 9: 1, 10: 2, 11: 3},
        compiler_params=params(),
        cost_estimate=cost(3 << 20),
    )(table, dirs, ghosts, far_rows, cells, rates, factor, boosts, outflow, new, keep, send)

    partner = lax.ppermute(send, "level", [(0, 1), (1, 0)])

    out = pl.pallas_call(
        write_kernel,
        name="ghost_write",
        in_specs=[SMEM, VMEM, HBM],
        out_specs=HBM,
        out_shape=jax.ShapeDtypeStruct((pipes * SEGF, columns), f32),
        scratch_shapes=[pltpu.SemaphoreType.DMA((pipes,))],
        input_output_aliases={2: 0},
        compiler_params=params(),
        cost_estimate=cost(4 << 20),
    )(ghosts, new, *pinned(pltpu.HBM, out))

    gap = pl.pallas_call(
        gap_kernel,
        name="level_gap",
        in_specs=[VMEM] * 2,
        out_specs=VMEM,
        out_shape=jax.ShapeDtypeStruct((pipes * 2, columns), f32),
        compiler_params=params(),
        cost_estimate=cost(1 << 20),
    )(keep, partner)
    return (out.reshape(1, pipes, SEGF, columns), gap.reshape(pipes, 2, columns))


def solution(mesh):
    in_specs = (
        P("level", "dom", None, "samp"),
        P("dom", None, "samp"),
        P("dom", None, "samp"),
        P("dom"),
        P("dom"),
        P("dom", None),
        P("dom"),
    )
    out_specs = (P("level", "dom", None, "samp"), P("dom", "level", "samp"))
    return jax.shard_map(
        per_device, mesh=mesh, in_specs=in_specs, out_specs=out_specs, check_vma=False
    )
```

profile of v0, /device:TPU:11, one launch (start us, length us, event | category | flops | bytes accessed | tf_op | source)
XLA Modules:
  0.0 30.2 jit_solution(9211180803524584502)
XLA Ops:
  0.6 0.0 copy-start
  0.6 3.5 %load_step.1 = (f32[8192,128]{1,0:T(8,128)S(1)}, f32[2048,128]{1,0:T(8,128)S(1)}, f32[3072,128]{1,0:T(8,128)S(1)}, f32[512,128]{1,0:T(8,128)S(1)}, f32[512,128]{...) custom-call(f32[8192,128]{1,0:T(8,128)} %bitcast.17, f32[2048,128]{1,0:T(8,128)} %bitcast.19, ...), custom_call_target="tpu_custom_call" | custom-call | bytes 5242880 | tf_op jit(solution)/shard_map/load_step/pallas_call | solution.py:362
  4.2 0.3 %collective-permute-start.1 = (f32[512,128]{1,0:T(8,128)S(1)}, f32[512,128]{1,0:T(8,128)S(1)}, u32[]{:S(2)}, u32[]{:S(2)}) collective-permute-start(f32[512,128]{1,0:T(8,128)S(1)} %get-tuple-element.24), channel_id=1, source_target_pairs={{0,2},{2,0},{4,6},{6,4},{8,10},{10,8},{12,14},{14,12},{1,3},{3,1},... | collective-permute-start | bytes 786440 | tf_op jit(solution)/shard_map/ppermute | solution.py:399
  4.5 4.1 %collective-permute-start = (f32[512,128]{1,0:T(8,128)S(1)}, f32[512,128]{1,0:T(8,128)S(1)}, u32[]{:S(2)}, u32[]{:S(2)}) collective-permute-start(f32[512,128]{1,0:T(8,128)S(1)} %get-tuple-element.24), channel_id=1, source_target_pairs={{2,4},{6,8},{10,12},{4,2},{8,6},{12,10},{3,5},{7,9},{11,13},{5,3},... | collective-permute-start | bytes 786440 | tf_op jit(solution)/shard_map/ppermute | solution.py:400
  8.6 0.0 copy-done
  8.7 9.7 %advance_step.1 = (f32[8192,128]{1,0:T(8,128)S(1)}, f32[8192,128]{1,0:T(8,128)}, f32[1024,128]{1,0:T(8,128)S(1)}, f32[1024,128]{1,0:T(8,128)S(1)}, s32[528]{0:T(1024)S(1)}) custom-call(s32[32,128]{1,0:T(8,128)S(1)} %get-tuple-element.17.table.refs_0_, s32[16,128]{1,0:T(8,128)S(1)} %bitcast.15, f32[8192,128]{1,0:T(8,128)S(1)} %get-tuple-element.18.cells.refs_4_, ...), custom_call_target="tpu_custom_call" | custom-call | bytes 20971520 | tf_op jit(solution)/shard_map/advance_step/pallas_call | solution.py:402
  18.3 0.0 collective-permute-done.1.refs_0_
  18.4 0.0 collective-permute-done.refs_3_
  18.4 3.3 %ghost_fix.1 = (f32[3072,128]{1,0:T(8,128)S(1)}, f32[8192,128]{1,0:T(8,128)S(1)}, f32[1024,128]{1,0:T(8,128)S(1)}, f32[1024,128]{1,0:T(8,128)S(1)}) custom-call(s32[32,128]{1,0:T(8,128)S(1)} %get-tuple-element.17.table.refs_0_, s32[16,128]{1,0:T(8,128)S(1)} %bitcast.16, ...), custom_call_target="tpu_custom_call", output_to_operand_aliasing={{0}: (8, {}), {1}: (9, {}), {2}: (10, {}), {3}: (11, {})} | custom-call | bytes 3145728 | tf_op jit(solution)/shard_map/ghost_fix/pallas_call | solution.py:431
  21.7 1.3 %collective-permute-start.2 = (f32[1024,128]{1,0:T(8,128)S(1)}, f32[1024,128]{1,0:T(8,128)S(1)}, u32[]{:S(2)}, u32[]{:S(2)}) collective-permute-start(f32[1024,128]{1,0:T(8,128)S(1)} %get-tuple-element.31), channel_id=1, source_target_pairs={{0,16},{16,0},{1,17},{17,1},{2,18},{18,2},{3,19},{19,3},{4,20},{20... | collective-permute-start | bytes 1572872 | tf_op jit(solution)/shard_map/ppermute | solution.py:448
  23.0 6.4 %ghost_write.1 = f32[8192,128]{1,0:T(8,128)} custom-call(s32[528]{0:T(1024)S(1)} %get-tuple-element.23.refs_2_.ghosts, f32[8192,128]{1,0:T(8,128)S(1)} %get-tuple-element.28.new, f32[8192,128]{1,0:T(8,128)} %get-tuple-element.29.out_in), custom_call_target="tpu_custom_call", output_to_operand_aliasing={{}: (2, {})} | custom-call | bytes 4194304 | tf_op jit(solution)/shard_map/ghost_write/pallas_call | solution.py:450
  29.4 0.0 collective-permute-done.2.partner
  29.4 0.9 %level_gap.1 = f32[1024,128]{1,0:T(8,128)} custom-call(f32[1024,128]{1,0:T(8,128)S(1)} %get-tuple-element.30.keep, f32[1024,128]{1,0:T(8,128)S(1)} %collective-permute-done.2.partner), custom_call_target="tpu_custom_call" | custom-call | bytes 1048576 | tf_op jit(solution)/shard_map/level_gap/pallas_call | solution.py:462
  (1 shorter events, 0.0 us)
Async XLA Ops:
  0.6 8.0 %copy-start = (s32[512,4,1]{0,2,1:T(1,128)S(1)}, s32[512,4,1]{0,2,1:T(1,128)}, u32[]{:S(2)}) copy-start(s32[512,4,1]{0,2,1:T(1,128)} %param.9) | copy-start | bytes 24580
  4.2 14.2 %collective-permute-start.1 = (f32[512,128]{1,0:T(8,128)S(1)}, f32[512,128]{1,0:T(8,128)S(1)}, u32[]{:S(2)}, u32[]{:S(2)}) collective-permute-start(f32[512,128]{1,0:T(8,128)S(1)} %get-tuple-element.24), channel_id=1, source_target_pairs={{0,2},{2,0},{4,6},{6,4},{8,10},{10,8},{12,14},{14,12},{1,3},{3,1},... | collective-permute-start | bytes 786440 | tf_op jit(solution)/shard_map/ppermute | solution.py:399
  4.5 13.9 %collective-permute-start = (f32[512,128]{1,0:T(8,128)S(1)}, f32[512,128]{1,0:T(8,128)S(1)}, u32[]{:S(2)}, u32[]{:S(2)}) collective-permute-start(f32[512,128]{1,0:T(8,128)S(1)} %get-tuple-element.24), channel_id=1, source_target_pairs={{2,4},{6,8},{10,12},{4,2},{8,6},{12,10},{3,5},{7,9},{11,13},{5,3},... | collective-permute-start | bytes 786440 | tf_op jit(solution)/shard_map/ppermute | solution.py:400
  21.7 7.7 %collective-permute-start.2 = (f32[1024,128]{1,0:T(8,128)S(1)}, f32[1024,128]{1,0:T(8,128)S(1)}, u32[]{:S(2)}, u32[]{:S(2)}) collective-permute-start(f32[1024,128]{1,0:T(8,128)S(1)} %get-tuple-element.31), channel_id=1, source_target_pairs={{0,16},{16,0},{1,17},{17,1},{2,18},{18,2},{3,19},{19,3},{4,20},{20... | collective-permute-start | bytes 1572872 | tf_op jit(solution)/shard_map/ppermute | solution.py:448
where the time goes:
time: 30.3 us; the launch traced here: 30.2 us
  Pallas kernels  23.8 us (79%)
  starting transfers between devices  5.71 us (19%)
  between operations  0.72 us (2%)
    pallas_call x1, Pallas kernels, per_device(): pl.pallas_call(step_kernel, name='advance_step', in_specs=[SMEM] * 2 + [V...  9.69 us
    pallas_call x1, Pallas kernels, per_device(): pl.pallas_call(write_kernel, name='ghost_write', in_specs=[SMEM, VMEM, HB...  6.37 us
    ppermute x1, starting transfers between devices, per_device(): far_rows = lax.ppermute(face_rows, 'dom', far_pairs)  4.12 us
    pallas_call x1, Pallas kernels, per_device(): pl.pallas_call(load_kernel, name='load_step', in_specs=[HBM] * 7, out_spe...  3.54 us
    pallas_call x1, Pallas kernels, per_device(): pl.pallas_call(lambda *refs: fix_kernel(first, *refs), name='ghost_fix',...  3.29 us
    ppermute x1, starting transfers between devices, per_device(): partner = lax.ppermute(send, 'level', [(0, 1), (1, 0)])  1.27 us
    pallas_call x1, Pallas kernels, per_device(): pl.pallas_call(gap_kernel, name='level_gap', in_specs=[VMEM] * 2, out_spe...  0.86 us
  transfers between devices with their start and end apart: 3, of which 0 were waited for; matrix products, arithmetic and copies ran while one was open for 0% of the time, Pallas kernels for 53%

commit v1 on v0

--- a/solution.py
+++ b/solution.py
@@ -157,41 +157,54 @@
             ]
 
 
-def fine_pipe(p, rev, src, cells, rates, outflow, factor, boosts, new):
-    near = pl.ds(pl.multiple_of(p * 16 + 8 * rev, 8), 8)
-    far = pl.ds(pl.multiple_of(p * 16 + 8 - 8 * rev, 8), 8)
+def fine_load(p, rev, src, cells, rates, outflow, factor, boosts):
     f = spread(factor, p)
-    b = f * spread(rates, p * 4)
+    r = spread(rates, p * 4)
+    bo = spread(boosts, p)
+    near = cells[pl.ds(pl.multiple_of(p * 16 + 8 * rev, 8), 8), :]
+    far = cells[pl.ds(pl.multiple_of(p * 16 + 8 - 8 * rev, 8), 8), :]
+    return f, r, bo, near, far, [spread(outflow, src + s) for s in range(GROUPS)]
+
+
+def fine_step(rev, loaded):
+    f, r, bo, near, far, inflow = loaded
+    b = f * r
     a = f - b
-    bo = spread(boosts, p)
-    y0, y1 = cells[near, :], cells[far, :]
+    edge = lax.broadcasted_iota(jnp.int32, (8, LANES), 0) == 7 * rev
     shift = 1 + 6 * rev
-    edge = lax.broadcasted_iota(jnp.int32, (8, LANES), 0) == 7 * rev
     for s in range(GROUPS):
-        inflow = spread(outflow, src + s) + bo
-        q0 = pltpu.roll(y0, shift, 0)
-        q1 = pltpu.roll(y1, shift, 0)
-        y1 = a * y1 + b * jnp.where(edge, q0, q1)
-        y0 = a * y0 + b * jnp.where(edge, inflow, q0)
-    new[near, :] = y0
-    new[far, :] = y1
-
-
-def coarse_pipe(p, srcs, codes, masks, cells, rates, outflow, factor, boosts, new):
-    low = lax.broadcasted_iota(jnp.int32, (8, LANES), 0) < 4
-    f = spread(factor, p)
-    bo = spread(boosts, p)
+        q0 = pltpu.roll(near, shift, 0)
+        q1 = pltpu.roll(far, shift, 0)
+        far = a * far + b * jnp.where(edge, q0, q1)
+        near = a * near + b * jnp.where(edge, inflow[s] + bo, q0)
+    return near, far
+
+
+def low_rows():
+    return lax.broadcasted_iota(jnp.int32, (8, LANES), 0) < 4
+
+
+def coarse_load(p, srcs, codes, masks, cells, rates, outflow, factor, boosts):
+    loaded = []
     for t in range(2):
-        own = pl.ds(pl.multiple_of(p * 16 + 8 * t, 8), 8)
-        x = cells[own, :]
-        r = jnp.where(low, spread(rates, p * 4 + 2 * t), spread(rates, p * 4 + 2 * t + 1))
-        inflow = jnp.where(low, spread(outflow, srcs[2 * t]), spread(outflow, srcs[2 * t + 1])) + bo
+        x = cells[pl.ds(pl.multiple_of(p * 16 + 8 * t, 8), 8), :]
+        r = [spread(rates, p * 4 + 2 * t + h) for h in range(2)]
+        inflow = [spread(outflow, srcs[2 * t + h]) for h in range(2)]
         code = pl.multiple_of(codes[t], 8)
-        turned = masks[pl.ds(code, 8), :] != 0.0
-        edge = masks[pl.ds(32 + code, 8), :] != 0.0
-        up = jnp.where(edge, inflow, jnp.where(turned, pltpu.roll(x, 7, 0), pltpu.roll(x, 1, 0)))
-        b = f * r
-        new[own, :] = (f - b) * x + b * up
+        loaded.append((x, r, inflow, masks[pl.ds(code, 8), :], masks[pl.ds(32 + code, 8), :]))
+    return spread(factor, p), spread(boosts, p), loaded
+
+
+def coarse_step(loaded):
+    f, bo, tiles = loaded
+    low = low_rows()
+    done = []
+    for x, r, inflow, turned, edge in tiles:
+        up = jnp.where(turned != 0.0, pltpu.roll(x, 7, 0), pltpu.roll(x, 1, 0))
+        up = jnp.where(edge != 0.0, jnp.where(low, inflow[0], inflow[1]) + bo, up)
+        b = f * jnp.where(low, r[0], r[1])
+        done.append((f - b) * x + b * up)
+    return done
 
 
 def fill_masks(masks):
@@ -203,66 +216,70 @@
         masks[32 + 8 * code : 40 + 8 * code, :] = edge.astype(jnp.float32)
 
 
-def one_pipe(fine, p, b, j, table, dirs, masks, *state):
-    blocks = dirs.shape[0] // GROUPS
-    if fine:
-        fine_pipe(p, dirs[b, j], table[b, j], *state)
-    else:
-        srcs = [table[g * blocks + b, j] for g in range(GROUPS)]
-        codes = [table[(GROUPS + t) * blocks + b, j] for t in range(2)]
-        coarse_pipe(p, srcs, codes, masks, *state)
+def shares(fine, k, q, new):
+    base = pl.multiple_of(q * 128, 128)
+    if not fine:
+        return new[pl.ds(base + k, 8, stride=16), :]
+    part = [new[pl.ds(base + 4 * k + i, 8, stride=16), :] for i in range(4)]
+    return ((part[0] + part[1]) + (part[2] + part[3])) * 0.25
 
 
 def step_kernel(
-    table, dirs, cells, rates, outflow, factor, boosts,
-    new, out, keep, send, ghosts,
-    masks, sems,
+    table, dirs, cells, rates, outflow, factor, boosts, new, send, ghosts, masks
 ):
     blocks = dirs.shape[0] // GROUPS
     level = lax.axis_index("level")
     fill_masks(masks)
-
-    def written(b):
-        part = pl.ds(pl.multiple_of(b * 16 * LANES, 128), 16 * LANES)
-        return pltpu.make_async_copy(new.at[part], out.at[part], sems.at[b])
+    state = (cells, rates, outflow, factor, boosts)
 
     def run(fine):
         def block(b, count):
             def some(m, count):
-                for u in range(8):
-                    j = m * 8 + u
-                    p = b * LANES + j
-                    one_pipe(
-                        fine, p, b, j, table, dirs, masks,
-                        cells, rates, outflow, factor, boosts, new,
-                    )
+                lanes = [m * 4 + u for u in range(4)]
+                pipes = [b * LANES + j for j in lanes]
+                for p, j in zip(pipes, lanes):
                     ghosts[count] = p
                     count = count + table[(GROUPS + 2) * blocks + b, j]
+                if fine:
+                    revs = [dirs[b, j] for j in lanes]
+                    loaded = [
+                        fine_load(p, rev, table[b, j], *state)
+                        for p, j, rev in zip(pipes, lanes, revs)
+                    ]
+                    done = [fine_step(rev, one) for rev, one in zip(revs, loaded)]
+                    for p, rev, (near, far) in zip(pipes, revs, done):
+                        new[pl.ds(pl.multiple_of(p * 16 + 8 * rev, 8), 8), :] = near
+                        new[pl.ds(pl.multiple_of(p * 16 + 8 - 8 * rev, 8), 8), :] = far
+                else:
+                    loaded = [
+                        coarse_load(
+                            p,
+                            [table[g * blocks + b, j] for g in range(GROUPS)],
+                            [table[(GROUPS + t) * blocks + b, j] for t in range(2)],
+                            masks,
+                            *state,
+                        )
+                        for p, j in zip(pipes, lanes)
+                    ]
+                    for p, one in zip(pipes, [coarse_step(one) for one in loaded]):
+                        for t in range(2):
+                            new[pl.ds(pl.multiple_of(p * 16 + 8 * t, 8), 8), :] = one[t]
                 return count
 
-            count = lax.fori_loop(0, LANES // 8, some, count)
-            written(b).start()
+            count = lax.fori_loop(0, LANES // 4, some, count)
 
             @pl.loop(0, LANES // 8)
             def _(m):
                 q = b * (LANES // 8) + m
-                base = pl.multiple_of(q * 128, 128)
-                for k in range(SEGC):
-                    if fine:
-                        part = [new[pl.ds(base + 4 * k + i, 8, stride=16), :] for i in range(4)]
-                        share = ((part[0] + part[1]) + (part[2] + part[3])) * 0.25
-                    else:
-                        share = new[pl.ds(base + k, 8, stride=16), :]
-                    dest = keep if (k < 2) == fine else send
-                    dest[pl.ds(pl.multiple_of(q * 16, 16) + k % 2, 8, stride=2), :] = share
+                for k in range(2):
+                    send[pl.ds(pl.multiple_of(q * 16, 16) + k, 8, stride=2), :] = shares(
+                        fine, k + 2 * fine, q, new
+                    )
 
             return count
 
         count = lax.fori_loop(0, blocks, block, jnp.int32(0))
-        last = ghosts[jnp.maximum(count - 1, 0)]
-        for u in range(8):
-            ghosts[count + u] = last
-        ghosts[blocks * LANES + 8] = count
+        ghosts[blocks * LANES] = count
 
     @pl.when(level == 0)
     def _():
@@ -272,11 +289,8 @@
     def _():
         run(False)
 
-    for b in range(blocks):
-        written(b).wait()
-
-
-def arrive_kernel(first, rows, near, arrived, outflow_in, outflow):
+
+def arrive_kernel(first, near, arrived, outflow_in, outflow):
     odd = lax.axis_index("dom") % 2
     half = arrived.shape[0]
     slot = 1 - odd if near else odd
@@ -285,35 +299,83 @@
 
 
 def fix_kernel(
-    first, table, dirs, ghosts, arrived, cells, rates, factor, boosts,
-    outflow_in, new_in, keep_in, send_in,
-    outflow, new, keep, send,
-    masks,
+    first, table, dirs, ghosts, arrived, rates, factor,
+    outflow_in, new_in, send_in, outflow, new, send, masks,
 ):
     blocks = dirs.shape[0] // GROUPS
     level = lax.axis_index("level")
-    arrive_kernel(first, 0, False, arrived, outflow_in, outflow)
+    arrive_kernel(first, False, arrived, outflow_in, outflow)
     fill_masks(masks)
-    count = ghosts[blocks * LANES + 8]
+    count = ghosts[blocks * LANES]
+    row = lax.broadcasted_iota(jnp.int32, (8, LANES), 0)
+
+    @pl.when(level == 0)
+    def _():
+        @pl.loop(0, count)
+        def _(i):
+            p = ghosts[i]
+            b, j = p // LANES, p % LANES
+            rev, src = dirs[b, j], table[b, j]
+            f = spread(factor, p)
+            beta = f * spread(rates, p * 4)
+            alpha = f - beta
+            edge = row == 7 * rev
+            shift = 1 + 6 * rev
+            delta = beta * jnp.where(edge, spread(outflow, src), 0.0)
+            for s in range(1, GROUPS):
+                up = jnp.where(edge, spread(outflow, src + s), pltpu.roll(delta, shift, 0))
+                delta = alpha * delta + beta * up
+            near = pl.ds(pl.multiple_of(p * 16 + 8 * rev, 8), 8)
+            new[near, :] = new[near, :] + delta
+
+            @pl.when(rev == 1)
+            def _():
+                own = pl.ds(p * 2 + 1, 1)
+                send[own, :] = send[own, :] + jnp.sum(delta, axis=0, keepdims=True) * 0.25
+
+    @pl.when(level == 1)
+    def _():
+        @pl.loop(0, count)
+        def _(i):
+            p = ghosts[i]
+            b, j = p // LANES, p % LANES
+            f = spread(factor, p)
+            low = row < 4
+            for t in range(2):
+                code = pl.multiple_of(table[(GROUPS + t) * blocks + b, j], 8)
+                edge = masks[pl.ds(32 + code, 8), :] != 0.0
+                terms = []
+                for g in (2 * t, 2 * t + 1):
+                    src = table[g * blocks + b, j]
+                    fed = jnp.where(src >= first, jnp.float32(1.0), jnp.float32(0.0))
+                    terms.append(spread(rates, p * 4 + g) * spread(outflow, src) * fed)
+                own = pl.ds(pl.multiple_of(p * 16 + 8 * t, 8), 8)
+                both = jnp.where(low, terms[0], terms[1])
+                tile = new[own, :] + jnp.where(edge, f * both, 0.0)
+                new[own, :] = tile
+                if t == 0:
+                    send[pl.ds(p * 2, 2), :] = tile[0:2]
+
+
+def keep_kernel(new, keep, out, sems):
+    level = lax.axis_index("level")
+    rows = new.shape[0] // sems.shape[0]
+    copies = []
+    for n in range(sems.shape[0]):
+        part = pl.ds(n * rows, rows)
+        copies.append(pltpu.make_async_copy(new.at[part], out.at[part], sems.at[n]))
+    for copy in copies:
+        copy.start()
 
     def run(fine):
-        @pl.loop(0, (count + 3) // 4)
+        @pl.loop(0, new.shape[0] // 256)
         def _(m):
-            pipes = [ghosts[m * 4 + u] for u in range(4)]
-            for p in pipes:
-                one_pipe(
-                    fine, p, p // LANES, p % LANES, table, dirs, masks,
-                    cells, rates, outflow, factor, boosts, new,
-                )
-            for p in pipes:
-                if fine:
-                    part = [new[pl.ds(p * 16 + i, 4, stride=4), :] for i in range(4)]
-                    share = ((part[0] + part[1]) + (part[2] + part[3])) * 0.25
-                else:
-                    share = new[pl.ds(pl.multiple_of(p * 16, 16), 4), :]
-                own = pl.ds(p * 2, 2)
-                keep[own, :] = share[0:2] if fine else share[2:4]
-                send[own, :] = share[2:4] if fine else share[0:2]
+            for u in range(2):
+                q = m * 2 + u
+                for k in range(2):
+                    keep[pl.ds(pl.multiple_of(q * 16, 16) + k, 8, stride=2), :] = shares(
+                        fine, k + 2 * (not fine), q, new
+                    )
 
     @pl.when(level == 0)
     def _():
@@ -322,28 +384,14 @@
     @pl.when(level == 1)
     def _():
         run(False)
+
+    for copy in copies:
+        copy.wait()
 
 
 def gap_kernel(keep, partner, gap):
     sign = jnp.where(lax.axis_index("level") == 0, jnp.float32(1.0), jnp.float32(-1.0))
     gap[...] = (keep[...] - partner[...]) * sign
-
-
-def write_kernel(ghosts, new, out_in, out, sems):
-    pipes = new.shape[0] // SEGF
-    count = ghosts[pipes + 8]
-
-    def moved(i):
-        part = pl.ds(pl.multiple_of(ghosts[i] * 16, 16), 16)
-        return pltpu.make_async_copy(new.at[part], out.at[part], sems.at[i])
-
-    @pl.loop(0, count)
-    def _(i):
-        moved(i).start()
-
-    @pl.loop(0, count)
-    def _(i):
-        moved(i).wait()
 
 
 def per_device(panels, courant, direction, decay, booster, feeder, face_index):
@@ -399,26 +447,24 @@
     near_rows = lax.ppermute(face_rows, "dom", near_pairs)
     far_rows = lax.ppermute(face_rows, "dom", far_pairs)
 
-    new, out, keep, send, ghosts = pl.pallas_call(
+    new, send, ghosts = pl.pallas_call(
         step_kernel,
         name="advance_step",
         in_specs=[SMEM] * 2 + [VMEM] * 5,
-        out_specs=[VMEM, HBM, VMEM, VMEM, SMEM],
+        out_specs=[VMEM, VMEM, SMEM],
         out_shape=[
             pltpu.VMEM((pipes * SEGF, columns), f32),
-            jax.ShapeDtypeStruct((pipes * SEGF, columns), f32),
-            pltpu.VMEM((pipes * 2, columns), f32),
             pltpu.VMEM((pipes * 2, columns), f32),
             jax.ShapeDtypeStruct((pipes + 16,), i32),
         ],
-        scratch_shapes=[pltpu.VMEM((64, columns), f32), pltpu.SemaphoreType.DMA((blocks,))],
+        scratch_shapes=[pltpu.VMEM((64, columns), f32)],
         compiler_params=params(),
         cost_estimate=cost(20 << 20),
     )(table, dirs, cells, rates, outflow, factor, boosts)
 
     first = GROUPS * pipes
     outflow = pl.pallas_call(
-        lambda *refs: arrive_kernel(first, 0, True, *refs),
+        lambda *refs: arrive_kernel(first, True, *refs),
         name="near_arrive",
         in_specs=[VMEM] * 2,
         out_specs=VMEM,
@@ -428,36 +474,37 @@
         cost_estimate=cost(1 << 19),
     )(near_rows, outflow)
 
-    outflow, new, keep, send = pl.pallas_call(
+    outflow, new, send = pl.pallas_call(
         lambda *refs: fix_kernel(first, *refs),
         name="ghost_fix",
-        in_specs=[SMEM] * 3 + [VMEM] * 9,
-        out_specs=[VMEM] * 4,
+        in_specs=[SMEM] * 3 + [VMEM] * 6,
+        out_specs=[VMEM] * 3,
         out_shape=[
             pltpu.VMEM((ghost_rows, columns), f32),
             pltpu.VMEM((pipes * SEGF, columns), f32),
             pltpu.VMEM((pipes * 2, columns), f32),
-            pltpu.VMEM((pipes * 2, columns), f32),
         ],
         scratch_shapes=[pltpu.VMEM((64, columns), f32)],
-        input_output_aliases={8: 0, 9: 1, 10: 2, 11: 3},
+        input_output_aliases={6: 0, 7: 1, 8: 2},
         compiler_params=params(),
         cost_estimate=cost(3 << 20),
-    )(table, dirs, ghosts, far_rows, cells, rates, factor, boosts, outflow, new, keep, send)
+    )(table, dirs, ghosts, far_rows, rates, factor, outflow, new, send)
 
     partner = lax.ppermute(send, "level", [(0, 1), (1, 0)])
 
-    out = pl.pallas_call(
-        write_kernel,
-        name="ghost_write",
-        in_specs=[SMEM, VMEM, HBM],
-        out_specs=HBM,
-        out_shape=jax.ShapeDtypeStruct((pipes * SEGF, columns), f32),
-        scratch_shapes=[pltpu.SemaphoreType.DMA((pipes,))],
-        input_output_aliases={2: 0},
+    keep, out = pl.pallas_call(
+        keep_kernel,
+        name="keep_share",
+        in_specs=[VMEM],
+        out_specs=[VMEM, HBM],
+        out_shape=[
+            pltpu.VMEM((pipes * 2, columns), f32),
+            jax.ShapeDtypeStruct((pipes * SEGF, columns), f32),
+        ],
+        scratch_shapes=[pltpu.SemaphoreType.DMA((4,))],
         compiler_params=params(),
         cost_estimate=cost(4 << 20),
-    )(ghosts, new, *pinned(pltpu.HBM, out))
+    )(new)
 
     gap = pl.pallas_call(
         gap_kernel,

time: 30.3 us -> 26.3 us (0.87)
  the two profiles are of different devices: /device:TPU:11 before, /device:TPU:7 now
where the time goes in v1:
time: 26.3 us; the launch traced here: 26 us
  Pallas kernels  20 us (76%)
  starting transfers between devices  5.35 us (20%)
  between operations  0.72 us (3%)
    pallas_call x1, Pallas kernels, per_device(): pl.pallas_call(step_kernel, name='advance_step', in_specs=[SMEM] * 2 + [V...  10.1 us
    ppermute x1, starting transfers between devices, per_device(): far_rows = lax.ppermute(face_rows, 'dom', far_pairs)  4.12 us
    pallas_call x1, Pallas kernels, per_device(): pl.pallas_call(load_kernel, name='load_step', in_specs=[HBM] * 7, out_spe...  3.54 us
    pallas_call x1, Pallas kernels, per_device(): pl.pallas_call(lambda *refs: fix_kernel(first, *refs), name='ghost_fix',...  3.37 us
    pallas_call x1, Pallas kernels, per_device(): pl.pallas_call(keep_kernel, name='keep_share', in_specs=[VMEM], out_specs...  2.04 us
    ppermute x1, starting transfers between devices, per_device(): partner = lax.ppermute(send, 'level', [(0, 1), (1, 0)])  0.91 us
    pallas_call x1, Pallas kernels, per_device(): pl.pallas_call(gap_kernel, name='level_gap', in_specs=[VMEM] * 2, out_spe...  0.85 us
  transfers between devices with their start and end apart: 3, of which 0 were waited for; matrix products, arithmetic and copies ran while one was open for 0% of the time, Pallas kernels for 47%

profile of v1, /device:TPU:7, one launch (start us, length us, event | category | flops | bytes accessed | tf_op | source)
XLA Modules:
  0.0 26.0 jit_solution(12807838601266496054)
XLA Ops:
  0.6 0.0 copy-start
  0.6 3.5 %load_step.1 = (f32[8192,128]{1,0:T(8,128)S(1)}, f32[2048,128]{1,0:T(8,128)S(1)}, f32[3072,128]{1,0:T(8,128)S(1)}, f32[512,128]{1,0:T(8,128)S(1)}, f32[512,128]{...) custom-call(f32[8192,128]{1,0:T(8,128)} %bitcast.17, f32[2048,128]{1,0:T(8,128)} %bitcast.18, ...), custom_call_target="tpu_custom_call" | custom-call | bytes 5242880 | tf_op jit(solution)/shard_map/load_step/pallas_call | solution.py:410
  4.2 0.3 %collective-permute-start.1 = (f32[512,128]{1,0:T(8,128)S(1)}, f32[512,128]{1,0:T(8,128)S(1)}, u32[]{:S(2)}, u32[]{:S(2)}) collective-permute-start(f32[512,128]{1,0:T(8,128)S(1)} %get-tuple-element.23), channel_id=1, source_target_pairs={{0,2},{2,0},{4,6},{6,4},{8,10},{10,8},{12,14},{14,12},{1,3},{3,1},... | collective-permute-start | bytes 786440 | tf_op jit(solution)/shard_map/ppermute | solution.py:447
  4.5 4.1 %collective-permute-start = (f32[512,128]{1,0:T(8,128)S(1)}, f32[512,128]{1,0:T(8,128)S(1)}, u32[]{:S(2)}, u32[]{:S(2)}) collective-permute-start(f32[512,128]{1,0:T(8,128)S(1)} %get-tuple-element.23), channel_id=1, source_target_pairs={{2,4},{6,8},{10,12},{4,2},{8,6},{12,10},{3,5},{7,9},{11,13},{5,3},... | collective-permute-start | bytes 786440 | tf_op jit(solution)/shard_map/ppermute | solution.py:448
  8.6 0.0 copy-done
  8.7 10.1 %advance_step.1 = (f32[8192,128]{1,0:T(8,128)S(1)}, f32[1024,128]{1,0:T(8,128)S(1)}, s32[528]{0:T(1024)S(1)}) custom-call(s32[32,128]{1,0:T(8,128)S(1)} %get-tuple-element.16.table.refs_0_, s32[16,128]{1,0:T(8,128)S(1)} %bitcast.15, f32[8192,128]{1,0:T(8,128)S(1)} %get-tuple-element.17.cells, f32[2048,128]{1,0:T(8,128)S(1)} %get-tuple-element.18.rates.refs_4_, ...), custom_call_target="tpu_custom_call" | custom-call | bytes 20971520 | tf_op jit(solution)/shard_map/advance_step/pallas_call | solution.py:450
  18.8 0.0 collective-permute-done.1.refs_0_
  18.8 0.0 collective-permute-done.refs_3_
  18.8 3.4 %ghost_fix.1 = (f32[3072,128]{1,0:T(8,128)S(1)}, f32[8192,128]{1,0:T(8,128)S(1)}, f32[1024,128]{1,0:T(8,128)S(1)}) custom-call(s32[32,128]{1,0:T(8,128)S(1)} %get-tuple-element.16.table.refs_0_, s32[16,128]{1,0:T(8,128)S(1)} %bitcast.16, s32[528]{0:T(1024)S(1)} %get-tuple-element.22.refs_2_, ...), custom_call_target="tpu_custom_call", output_to_operand_aliasing={{0}: (6, {}), {1}: (7, {}), {2}: (8, {})} | custom-call | bytes 3145728 | tf_op jit(solution)/shard_map/ghost_fix/pallas_call | solution.py:477
  22.2 0.9 %collective-permute-start.2 = (f32[1024,128]{1,0:T(8,128)S(1)}, f32[1024,128]{1,0:T(8,128)S(1)}, u32[]{:S(2)}, u32[]{:S(2)}) collective-permute-start(f32[1024,128]{1,0:T(8,128)S(1)} %get-tuple-element.29), channel_id=1, source_target_pairs={{0,16},{16,0},{1,17},{17,1},{2,18},{18,2},{3,19},{19,3},{4,20},{20... | collective-permute-start | bytes 1572872 | tf_op jit(solution)/shard_map/ppermute | solution.py:493
  23.1 2.0 %keep_share.1 = (f32[1024,128]{1,0:T(8,128)S(1)}, f32[8192,128]{1,0:T(8,128)}) custom-call(f32[8192,128]{1,0:T(8,128)S(1)} %get-tuple-element.26.new), custom_call_target="tpu_custom_call" | custom-call | bytes 4194304 | tf_op jit(solution)/shard_map/keep_share/pallas_call | solution.py:495
  25.2 0.0 collective-permute-done.2.partner
  25.2 0.8 %level_gap.1 = f32[1024,128]{1,0:T(8,128)} custom-call(f32[1024,128]{1,0:T(8,128)S(1)} %get-tuple-element.28.keep, f32[1024,128]{1,0:T(8,128)S(1)} %collective-permute-done.2.partner), custom_call_target="tpu_custom_call" | custom-call | bytes 1048576 | tf_op jit(solution)/shard_map/level_gap/pallas_call | solution.py:509
  (1 shorter events, 0.0 us)
Async XLA Ops:
  0.6 8.0 %copy-start = (s32[512,4,1]{0,2,1:T(1,128)S(1)}, s32[512,4,1]{0,2,1:T(1,128)}, u32[]{:S(2)}) copy-start(s32[512,4,1]{0,2,1:T(1,128)} %param.9) | copy-start | bytes 24580
  4.2 14.6 %collective-permute-start.1 = (f32[512,128]{1,0:T(8,128)S(1)}, f32[512,128]{1,0:T(8,128)S(1)}, u32[]{:S(2)}, u32[]{:S(2)}) collective-permute-start(f32[512,128]{1,0:T(8,128)S(1)} %get-tuple-element.23), channel_id=1, source_target_pairs={{0,2},{2,0},{4,6},{6,4},{8,10},{10,8},{12,14},{14,12},{1,3},{3,1},... | collective-permute-start | bytes 786440 | tf_op jit(solution)/shard_map/ppermute | solution.py:447
  4.5 14.3 %collective-permute-start = (f32[512,128]{1,0:T(8,128)S(1)}, f32[512,128]{1,0:T(8,128)S(1)}, u32[]{:S(2)}, u32[]{:S(2)}) collective-permute-start(f32[512,128]{1,0:T(8,128)S(1)} %get-tuple-element.23), channel_id=1, source_target_pairs={{2,4},{6,8},{10,12},{4,2},{8,6},{12,10},{3,5},{7,9},{11,13},{5,3},... | collective-permute-start | bytes 786440 | tf_op jit(solution)/shard_map/ppermute | solution.py:448
  22.2 3.0 %collective-permute-start.2 = (f32[1024,128]{1,0:T(8,128)S(1)}, f32[1024,128]{1,0:T(8,128)S(1)}, u32[]{:S(2)}, u32[]{:S(2)}) collective-permute-start(f32[1024,128]{1,0:T(8,128)S(1)} %get-tuple-element.29), channel_id=1, source_target_pairs={{0,16},{16,0},{1,17},{17,1},{2,18},{18,2},{3,19},{19,3},{4,20},{20... | collective-permute-start | bytes 1572872 | tf_op jit(solution)/shard_map/ppermute | solution.py:493

commit v2 on v0

v2 whole, which is shorter than its diff:
```python
import jax
import jax.numpy as jnp
from jax import lax
from jax.experimental import pallas as pl
from jax.experimental.pallas import tpu as pltpu
from jax.sharding import PartitionSpec as P

SEGF = 16
SEGC = 4
GROUPS = SEGF // SEGC
LANES = 128
CHUNKS = 4
MARK = -(1 << 31)

HBM = pl.BlockSpec(memory_space=pltpu.HBM)
VMEM = pl.BlockSpec(memory_space=pltpu.VMEM)
SMEM = pl.BlockSpec(memory_space=pltpu.SMEM)


def params():
    return pltpu.CompilerParams(vmem_limit_bytes=8 << 20)


def cost(nbytes):
    return pl.CostEstimate(flops=0, bytes_accessed=nbytes, transcendentals=0)


def pinned(space, *arrays):
    return [pltpu.with_memory_space_constraint(x, space) for x in arrays]


def down_rows(row):
    return jnp.broadcast_to(row, (LANES, LANES)).T


def spread(ref, row):
    return ref[pl.ds(row, 8, stride=0), :]


def load_kernel(
    panel, rate, dirs, feed, decay, boost, faces,
    cells, rates, outflow, factor, boosts, flow_back, words, face_rows,
    dir_v, feed_v, decay_v, boost_v, face_s, panel_sem, rate_sem, small_sem,
):
    rows = panel.shape[0] // CHUNKS
    blocks = decay.shape[0]
    pipes = blocks * LANES
    level = lax.axis_index("level")

    def chunk(n):
        part = pl.ds(pl.multiple_of(n * rows, rows), rows)
        return pltpu.make_async_copy(panel.at[part], cells.at[part], panel_sem.at[n])

    small = [
        pltpu.make_async_copy(src, dst, small_sem.at[n])
        for n, (src, dst) in enumerate(
            ((dirs, dir_v), (feed, feed_v), (decay, decay_v), (boost, boost_v), (faces, face_s))
        )
    ]
    rate_copy = pltpu.make_async_copy(rate, rates, rate_sem)
    for copy in small:
        copy.start()
    rate_copy.start()
    for n in range(CHUNKS):
        chunk(n).start()
    for copy in small:
        copy.wait()

    scale = jnp.where(level == 0, jnp.float32(-0.25), jnp.float32(-1.0))
    fac = jnp.exp(decay_v[...] * scale)
    for b in range(blocks):
        own = slice(b * LANES, (b + 1) * LANES)
        factor[own, :] = down_rows(fac[b : b + 1])
        boosts[own, :] = down_rows(boost_v[b : b + 1])
    outflow[GROUPS * pipes :, :] = jnp.zeros_like(outflow[GROUPS * pipes :, :])
    back = (dir_v[...] == 1).astype(jnp.int32)
    lane = lax.broadcasted_iota(jnp.int32, (1, LANES), 1)
    for b in range(blocks):
        ahead = feed_v[2 * b : 2 * b + 1, :]
        behind = feed_v[2 * b + 1 : 2 * b + 2, :]
        rev = back[b : b + 1, :]
        src = jnp.where(rev == 1, behind, ahead)
        p = lane + b * LANES
        fine = src + (p << 10) + (rev << 20) + jnp.where(src >= pipes, MARK, 0)
        fed = jnp.maximum(ahead, behind) >= pipes
        coarse = ahead + (behind << 10) + (p << 20) + jnp.where(fed, MARK, 0)
        words[b : b + 1, :] = jnp.where(level == 0, fine, coarse)
    backf = back.astype(jnp.float32)

    def back_rows(g):
        for b in range(blocks):
            at = g * blocks + b
            flow_back[at * LANES : (at + 1) * LANES, :] = down_rows(backf[at : at + 1])

    back_rows(0)

    @pl.when(level == 1)
    def _():
        for g in range(1, GROUPS):
            back_rows(g)

    rate_copy.wait()
    per_chunk = pipes // 8 // CHUNKS

    @pl.when(level == 0)
    def _():
        @pl.loop(0, CHUNKS)
        def _(n):
            chunk(n).wait()
            for i in range(per_chunk):
                q = n * per_chunk + i
                base = pl.multiple_of(q * 128, 128)
                own = pl.ds(pl.multiple_of(q * 8, 8), 8)
                rev = flow_back[own, :] != 0.0
                b = factor[own, :] * rates[pl.ds(pl.multiple_of(q * 32, 32), 8, stride=4), :]
                a = factor[own, :] - b
                y = [
                    jnp.where(
                        rev,
                        cells[pl.ds(base + j, 8, stride=16), :],
                        cells[pl.ds(base + 15 - j, 8, stride=16), :],
                    )
                    for j in range(GROUPS)
                ]
                for s in range(GROUPS):
                    outflow[pl.ds(pl.multiple_of(q * 32, 32) + s, 8, stride=4), :] = y[0]
                    y = [a * y[j] + b * y[j + 1] for j in range(len(y) - 1)]

    @pl.when(level == 1)
    def _():
        @pl.loop(0, CHUNKS)
        def _(n):
            chunk(n).wait()
            for i in range(per_chunk):
                q = n * per_chunk + i
                base = pl.multiple_of(q * 128, 128)
                for g in range(GROUPS):
                    rev = flow_back[pl.ds(pl.multiple_of(g * pipes + q * 8, 8), 8), :] != 0.0
                    outflow[pl.ds(pl.multiple_of(q * 32, 32) + g, 8, stride=4), :] = jnp.where(
                        rev,
                        cells[pl.ds(base + 4 * g, 8, stride=16), :],
                        cells[pl.ds(base + 4 * g + 3, 8, stride=16), :],
                    )

    @pl.loop(0, faces.shape[0] // 8)
    def _(m):
        for u in range(8):
            pipe = face_s[m * 8 + u]
            face_rows[pl.ds(pl.multiple_of(m * 32, 32) + 4 * u, 4), :] = outflow[
                pl.ds(pl.multiple_of(pipe * 4, 4), 4), :
            ]


def eight_words(q, words):
    per = LANES // 8
    return [words[q // per, (q % per) * 8 + u] for u in range(8)]


def gather_eight(fine, q, words, outflow, ahead_in, behind_in):
    start = pl.multiple_of(q * 32, 32)
    entries = eight_words(q, words)
    moved = [[outflow[pl.ds(pl.multiple_of((w & 1023) * 4, 4), 4), :] for w in entries]]
    if not fine:
        moved.append(
            [outflow[pl.ds(pl.multiple_of((w >> 10 & 1023) * 4, 4), 4), :] for w in entries]
        )
    for dest, tiles in zip((ahead_in, behind_in), moved):
        for u in range(8):
            dest[pl.ds(start + 4 * u, 4), :] = tiles[u]


def list_eight(q, words, ghosts, count):
    for w in eight_words(q, words):
        ghosts[count] = w
        count = count + lax.shift_right_logical(w, 31)
    return count


def fine_block(q, cells, rates, factor, boosts, flow_back, ahead_in, new, keep, send):
    own = pl.ds(pl.multiple_of(q * 8, 8), 8)
    base = pl.multiple_of(q * 128, 128)
    quad = pl.multiple_of(q * 32, 32)
    pair = pl.multiple_of(q * 16, 16)
    rev = flow_back[own, :] != 0.0
    f = factor[own, :]
    b = f * rates[pl.ds(quad, 8, stride=4), :]
    a = f - b
    bo = boosts[own, :]
    x = [cells[pl.ds(base + k, 8, stride=16), :] for k in range(SEGF)]
    o = [jnp.where(rev, x[SEGF - 1 - k], x[k]) for k in range(SEGF)]
    for s in range(GROUPS):
        inflow = ahead_in[pl.ds(quad + s, 8, stride=4), :] + bo
        o = [a * o[k] + b * (o[k - 1] if k else inflow) for k in range(SEGF)]
    y = [jnp.where(rev, o[SEGF - 1 - k], o[k]) for k in range(SEGF)]
    for k in range(SEGF):
        new[pl.ds(base + k, 8, stride=16), :] = y[k]
    for k in range(SEGC):
        share = ((y[4 * k] + y[4 * k + 1]) + (y[4 * k + 2] + y[4 * k + 3])) * 0.25
        (keep if k < 2 else send)[pl.ds(pair + k % 2, 8, stride=2), :] = share


def coarse_block(
    q, cells, rates, factor, boosts, flow_back, ahead_in, behind_in, new, keep, send
):
    pipes = factor.shape[0]
    own = pl.ds(pl.multiple_of(q * 8, 8), 8)
    base = pl.multiple_of(q * 128, 128)
    quad = pl.multiple_of(q * 32, 32)
    pair = pl.multiple_of(q * 16, 16)
    f = factor[own, :]
    bo = boosts[own, :]
    for g in range(GROUPS):
        rev = flow_back[pl.ds(pl.multiple_of(g * pipes + q * 8, 8), 8), :] != 0.0
        four = pl.ds(quad + g, 8, stride=4)
        b = f * rates[four, :]
        a = f - b
        inflow = jnp.where(rev, behind_in[four, :], ahead_in[four, :]) + bo
        x = [cells[pl.ds(base + 4 * g + k, 8, stride=16), :] for k in range(SEGC)]
        up = [
            jnp.where(
                rev, x[k + 1] if k + 1 < SEGC else inflow, x[k - 1] if k else inflow
            )
            for k in range(SEGC)
        ]
        y = [a * x[k] + b * up[k] for k in range(SEGC)]
        for k in range(SEGC):
            new[pl.ds(base + 4 * g + k, 8, stride=16), :] = y[k]
            if g == 0:
                (send if k < 2 else keep)[pl.ds(pair + k % 2, 8, stride=2), :] = y[k]


def step_kernel(
    words, cells, rates, outflow, factor, boosts, flow_back,
    new, keep, send, ghosts, ahead_in, behind_in,
):
    level = lax.axis_index("level")
    eights = factor.shape[0] // 8

    def run(fine):
        gather_eight(fine, 0, words, outflow, ahead_in, behind_in)

        def some(q, count):
            if fine:
                fine_block(q, cells, rates, factor, boosts, flow_back, ahead_in, new, keep, send)
            else:
                coarse_block(
                    q, cells, rates, factor, boosts, flow_back, ahead_in, behind_in,
                    new, keep, send,
                )
            later = jnp.minimum(q + 1, eights - 1)
            gather_eight(fine, later, words, outflow, ahead_in, behind_in)
            return list_eight(q, words, ghosts, count)

        ghosts[8 * eights] = lax.fori_loop(0, eights, some, jnp.int32(0))

    @pl.when(level == 0)
    def _():
        run(True)

    @pl.when(level == 1)
    def _():
        run(False)


def arrive_kernel(first, near, arrived, outflow_in, outflow):
    odd = lax.axis_index("dom") % 2
    half = arrived.shape[0]
    slot = 1 - odd if near else odd
    start = pl.multiple_of(first + slot * half, 8)
    outflow[pl.ds(start, half), :] = arrived[...]


def fine_fix(first, words, rates, factor, outflow, new, keep, send):
    row = lax.broadcasted_iota(jnp.int32, (8, LANES), 0)
    loaded = []
    for w in words:
        src, p, rev = w & 1023, w >> 10 & 1023, w >> 20 & 1
        near = pl.ds(pl.multiple_of(p * 16 + 8 * rev, 8), 8)
        kept, sent = pl.ds(p * 2, 1), pl.ds(p * 2 + 1, 1)
        inflow = [spread(outflow, src * 4 + s) for s in range(GROUPS)]
        loaded.append((
            rev, near, kept, sent, spread(factor, p), spread(rates, p * 4), inflow,
            new[near, :], keep[kept, :], send[sent, :],
        ))
    done = []
    for rev, near, kept, sent, f, r, inflow, tile, keep_row, send_row in loaded:
        b = f * r
        a = f - b
        edge = row == 7 * rev
        shift = 1 + 6 * rev
        total = b * inflow[0]
        delta = jnp.where(edge, total, 0.0)
        for s in range(1, GROUPS):
            up = jnp.where(edge, inflow[s], pltpu.roll(delta, shift, 0))
            delta = a * delta + b * up
            total = f * total + b * inflow[s]
        part = total[0:1] * 0.25
        back = jnp.where(rev == 1, jnp.float32(1.0), jnp.float32(0.0))
        done.append((
            near, kept, sent, tile + delta,
            keep_row + part * (1.0 - back), send_row + part * back,
        ))
    for near, kept, sent, tile, keep_row, send_row in done:
        new[near, :] = tile
        keep[kept, :] = keep_row
        send[sent, :] = send_row


def coarse_fix(first, words, rates, factor, flow_back, outflow, new, keep, send):
    pipes = factor.shape[0]
    zeros = outflow.shape[0] - 8
    loaded = []
    for w in words:
        p = w >> 20 & 1023
        rows = []
        for src in (w & 1023, w >> 10 & 1023):
            at = jnp.where(src >= pipes, src * 4, zeros)
            rows.append(outflow[pl.ds(pl.multiple_of(at, 4), 4), :])
        low = pl.ds(p * 16, 4, stride=4)
        high = pl.ds(p * 16 + 3, 4, stride=4)
        loaded.append((
            p, low, high, rows, flow_back[pl.ds(p, 4, stride=pipes), :],
            rates[pl.ds(pl.multiple_of(p * 4, 4), 4), :], factor[pl.ds(p, 4, stride=0), :],
            new[low, :], new[high, :],
        ))
    done = []
    for p, low, high, rows, rev, r, f, first_rows, last_rows in loaded:
        turned = rev != 0.0
        delta = f * r * jnp.where(turned, rows[1], rows[0])
        done.append((
            p, low, high,
            first_rows + jnp.where(turned, 0.0, delta), last_rows + jnp.where(turned, delta, 0.0),
        ))
    for p, low, high, first_rows, last_rows in done:
        new[low, :] = first_rows
        new[high, :] = last_rows
        send[pl.ds(p * 2, 1), :] = first_rows[0:1]
        keep[pl.ds(p * 2 + 1, 1), :] = last_rows[0:1]


def fix_kernel(
    first, ghosts, arrived, rates, factor, flow_back,
    outflow_in, new_in, keep_in, send_in, outflow, new, keep, send,
):
    level = lax.axis_index("level")
    arrive_kernel(first, False, arrived, outflow_in, outflow)
    count = ghosts[factor.shape[0]]

    def run(fix, *state):
        def some(start, width):
            at = [start + u for u in range(width)]
            fix(first, [ghosts[i] for i in at], *state)

        whole = count // 4

        @pl.loop(0, whole)
        def _(m):
            some(m * 4, 4)

        @pl.loop(whole * 4, count)
        def _(i):
            some(i, 1)

    @pl.when(level == 0)
    def _():
        run(fine_fix, rates, factor, outflow, new, keep, send)

    @pl.when(level == 1)
    def _():
        run(coarse_fix, rates, factor, flow_back, outflow, new, keep, send)


def write_kernel(new, out, sems):
    rows = new.shape[0] // sems.shape[0]
    copies = []
    for n in range(sems.shape[0]):
        part = pl.ds(n * rows, rows)
        copies.append(pltpu.make_async_copy(new.at[part], out.at[part], sems.at[n]))
    for copy in copies:
        copy.start()
    for copy in copies:
        copy.wait()


def gap_kernel(keep, partner, gap):
    sign = jnp.where(lax.axis_index("level") == 0, jnp.float32(1.0), jnp.float32(-1.0))
    gap[...] = (keep[...] - partner[...]) * sign


def per_device(panels, courant, direction, decay, booster, feeder, face_index):
    pipes = panels.shape[1]
    columns = panels.shape[3]
    faces = face_index.shape[0]
    blocks = pipes // LANES
    domains = lax.axis_size("dom")
    f32, i32 = jnp.float32, jnp.int32
    cells_in = panels.reshape(pipes * SEGF, columns)
    rates_in = courant.reshape(pipes * GROUPS, columns)
    dirs = direction.transpose(1, 2, 0).reshape(GROUPS * blocks, LANES)
    feed = feeder.reshape(blocks, LANES, 2).transpose(0, 2, 1).reshape(2 * blocks, LANES)
    ghost_rows = GROUPS * (pipes + 2 * faces) + 8

    cells, rates, outflow, factor, boosts, flow_back, words, face_rows = pl.pallas_call(
        load_kernel,
        name="load_step",
        in_specs=[HBM] * 7,
        out_specs=[VMEM] * 8,
        out_shape=[
            pltpu.VMEM((pipes * SEGF, columns), f32),
            pltpu.VMEM((pipes * GROUPS, columns), f32),
            pltpu.VMEM((ghost_rows, columns), f32),
            pltpu.VMEM((pipes, columns), f32),
            pltpu.VMEM((pipes, columns), f32),
            pltpu.VMEM((GROUPS * pipes, columns), f32),
            jax.ShapeDtypeStruct((blocks, LANES), i32),
            pltpu.VMEM((faces * GROUPS, columns), f32),
        ],
        scratch_shapes=[
            pltpu.VMEM(dirs.shape, i32),
            pltpu.VMEM(feed.shape, i32),
            pltpu.VMEM((blocks, LANES), f32),
            pltpu.VMEM((blocks, LANES), f32),
            pltpu.SMEM((faces,), i32),
            pltpu.SemaphoreType.DMA((CHUNKS,)),
            pltpu.SemaphoreType.DMA(()),
            pltpu.SemaphoreType.DMA((5,)),
        ],
        compiler_params=params(),
        cost_estimate=cost(5 << 20),
    )(
        *pinned(
            pltpu.HBM, cells_in, rates_in, dirs, feed,
            decay.reshape(blocks, LANES), booster.reshape(blocks, LANES), face_index,
        )
    )

    near_pairs = [(i, i ^ 1) for i in range(domains) if i ^ 1 < domains]
    far_pairs = [(i, i + 1) for i in range(1, domains - 1, 2)]
    far_pairs = far_pairs + [(j, i) for i, j in far_pairs]
    near_rows = lax.ppermute(face_rows, "dom", near_pairs)
    far_rows = lax.ppermute(face_rows, "dom", far_pairs)

    new, keep, send, ghosts = pl.pallas_call(
        step_kernel,
        name="advance_step",
        in_specs=[SMEM] + [VMEM] * 6,
        out_specs=[VMEM, VMEM, VMEM, SMEM],
        out_shape=[
            pltpu.VMEM((pipes * SEGF, columns), f32),
            pltpu.VMEM((pipes * 2, columns), f32),
            pltpu.VMEM((pipes * 2, columns), f32),
            pltpu.SMEM((pipes + 8,), i32),
        ],
        scratch_shapes=[pltpu.VMEM((GROUPS * pipes, columns), f32)] * 2,
        compiler_params=params(),
        cost_estimate=cost(20 << 20),
    )(words, cells, rates, outflow, factor, boosts, flow_back)

    first = GROUPS * pipes
    outflow = pl.pallas_call(
        lambda *refs: arrive_kernel(first, True, *refs),
        name="near_arrive",
        in_specs=[VMEM] * 2,
        out_specs=VMEM,
        out_shape=pltpu.VMEM((ghost_rows, columns), f32),
        input_output_aliases={1: 0},
        compiler_params=params(),
        cost_estimate=cost(1 << 19),
    )(near_rows, outflow)

    outflow, new, keep, send = pl.pallas_call(
        lambda *refs: fix_kernel(first, *refs),
        name="ghost_fix",
        in_specs=[SMEM] + [VMEM] * 8,
        out_specs=[VMEM] * 4,
        out_shape=[
            pltpu.VMEM((ghost_rows, columns), f32),
            pltpu.VMEM((pipes * SEGF, columns), f32),
            pltpu.VMEM((pipes * 2, columns), f32),
            pltpu.VMEM((pipes * 2, columns), f32),
        ],
        input_output_aliases={5: 0, 6: 1, 7: 2, 8: 3},
        compiler_params=params(),
        cost_estimate=cost(3 << 20),
    )(ghosts, far_rows, rates, factor, flow_back, outflow, new, keep, send)

    partner = lax.ppermute(send, "level", [(0, 1), (1, 0)])

    out = pl.pallas_call(
        write_kernel,
        name="write_cells",
        in_specs=[VMEM],
        out_specs=HBM,
        out_shape=jax.ShapeDtypeStruct((pipes * SEGF, columns), f32),
        scratch_shapes=[pltpu.SemaphoreType.DMA((4,))],
        compiler_params=params(),
        cost_estimate=cost(4 << 20),
    )(new)

    gap = pl.pallas_call(
        gap_kernel,
        name="level_gap",
        in_specs=[VMEM] * 2,
        out_specs=VMEM,
        out_shape=jax.ShapeDtypeStruct((pipes * 2, columns), f32),
        compiler_params=params(),
        cost_estimate=cost(1 << 20),
    )(keep, partner)
    return (out.reshape(1, pipes, SEGF, columns), gap.reshape(pipes, 2, columns))


def solution(mesh):
    in_specs = (
        P("level", "dom", None, "samp"),
        P("dom", None, "samp"),
        P("dom", None, "samp"),
        P("dom"),
        P("dom"),
        P("dom", None),
        P("dom"),
    )
    out_specs = (P("level", "dom", None, "samp"), P("dom", "level", "samp"))
    return jax.shard_map(
        per_device, mesh=mesh, in_specs=in_specs, out_specs=out_specs, check_vma=False
    )
```

time: 30.3 us -> 22.4 us (0.74)
  Pallas kernels: 23.8 us -> 13.9 us
  waiting for transfers between devices: 0.01 us -> 2.02 us
    pallas_call x3, Pallas kernels: 16.1 us -> 8.51 us  [the longest x1 6.44 us: per_device(): pl.pallas_call(step_kernel, name='advance_step', in_specs=[SMEM] + [VMEM]...]
    pallas_call x1, Pallas kernels: 3.29 us -> 1.18 us  [per_device(): pl.pallas_call(lambda *refs: fix_kernel(first, *refs), name='ghost_fix',...]
    ppermute x1, waiting for transfers between devices: 0.01 us -> 2.02 us  [per_device(): near_rows = lax.ppermute(face_rows, 'dom', near_pairs)]
  transfers between devices with their start and end apart: 3 -> 3, of which waited for: 0 -> 1; matrix products, arithmetic and copies ran while one was open for 0% -> 0% of each run, Pallas kernels for 53% -> 38%
where the time goes in v2:
time: 22.4 us; the launch traced here: 22.1 us
  Pallas kernels  13.9 us (62%)
  starting transfers between devices  5.5 us (25%)
  waiting for transfers between devices  2.02 us (9%)
  between operations  0.7 us (3%)
    pallas_call x1, Pallas kernels, per_device(): pl.pallas_call(step_kernel, name='advance_step', in_specs=[SMEM] + [VMEM]...  6.44 us
    ppermute x1, starting transfers between devices, per_device(): far_rows = lax.ppermute(face_rows, 'dom', far_pairs)  4.12 us
    pallas_call x1, Pallas kernels, per_device(): pl.pallas_call(load_kernel, name='load_step', in_specs=[HBM] * 7, out_spe...  3.33 us
    pallas_call x1, Pallas kernels, per_device(): pl.pallas_call(write_kernel, name='write_cells', in_specs=[VMEM], out_spe...  2.04 us
    ppermute x1, waiting for transfers between devices, per_device(): near_rows = lax.ppermute(face_rows, 'dom', near_pairs)  2.02 us
    pallas_call x1, Pallas kernels, per_device(): pl.pallas_call(lambda *refs: fix_kernel(first, *refs), name='ghost_fix',...  1.18 us
    ppermute x1, starting transfers between devices, per_device(): partner = lax.ppermute(send, 'level', [(0, 1), (1, 0)])  1.06 us
    pallas_call x1, Pallas kernels, per_device(): pl.pallas_call(gap_kernel, name='level_gap', in_specs=[VMEM] * 2, out_spe...  0.85 us
  transfers between devices with their start and end apart: 3, of which 1 were waited for; matrix products, arithmetic and copies ran while one was open for 0% of the time, Pallas kernels for 38%

profile of v2, /device:TPU:11, one launch (start us, length us, event | category | flops | bytes accessed | tf_op | source)
XLA Modules:
  0.0 22.1 jit_solution(1328111050440106760)
XLA Ops:
  0.6 3.3 %load_step.1 = (f32[8192,128]{1,0:T(8,128)S(1)}, f32[2048,128]{1,0:T(8,128)S(1)}, f32[3080,128]{1,0:T(8,128)S(1)}, f32[512,128]{1,0:T(8,128)S(1)}, f32[512,128]{...) custom-call(f32[8192,128]{1,0:T(8,128)} %bitcast.14, ...), custom_call_target="tpu_custom_call" | custom-call | bytes 5242880 | tf_op jit(solution)/shard_map/load_step/pallas_call | solution.py:403
  4.0 0.3 %collective-permute-start.1 = (f32[512,128]{1,0:T(8,128)S(1)}, f32[512,128]{1,0:T(8,128)S(1)}, u32[]{:S(2)}, u32[]{:S(2)}) collective-permute-start(f32[512,128]{1,0:T(8,128)S(1)} %get-tuple-element.25), channel_id=1, source_target_pairs={{0,2},{2,0},{4,6},{6,4},{8,10},{10,8},{12,14},{14,12},{1,3},{3,1},... | collective-permute-start | bytes 786440 | tf_op jit(solution)/shard_map/ppermute | solution.py:440
  4.3 4.1 %collective-permute-start = (f32[512,128]{1,0:T(8,128)S(1)}, f32[512,128]{1,0:T(8,128)S(1)}, u32[]{:S(2)}, u32[]{:S(2)}) collective-permute-start(f32[512,128]{1,0:T(8,128)S(1)} %get-tuple-element.25), channel_id=1, source_target_pairs={{2,4},{6,8},{10,12},{4,2},{8,6},{12,10},{3,5},{7,9},{11,13},{5,3},... | collective-permute-start | bytes 786440 | tf_op jit(solution)/shard_map/ppermute | solution.py:441
  8.4 6.4 %advance_step.1 = (f32[8192,128]{1,0:T(8,128)S(1)}, f32[1024,128]{1,0:T(8,128)S(1)}, f32[1024,128]{1,0:T(8,128)S(1)}, s32[520]{0:T(1024)S(4)}) custom-call(s32[4,128]{1,0:T(4,128)S(1)} %get-tuple-element.17.words, f32[8192,128]{1,0:T(8,128)S(1)} %get-tuple-element.18.cells, f32[2048,128]{1,0:T(8,128)S(1)} %get-tuple-element.19.rates.refs_2_, ...), custom_call_target="tpu_custom_call" | custom-call | bytes 20971520 | tf_op jit(solution)/shard_map/advance_step/pallas_call | solution.py:443
  14.9 2.0 %collective-permute-done.1.refs_0_ = f32[512,128]{1,0:T(8,128)S(1)} collective-permute-done((f32[512,128]{1,0:T(8,128)S(1)}, f32[512,128]{1,0:T(8,128)S(1)}, u32[]{:S(2)}, u32[]{:S(2)}) %collective-permute-start.1) | collective-permute-done | bytes 262176 | tf_op jit(solution)/shard_map/ppermute | solution.py:440
  16.9 0.0 collective-permute-done.refs_1_
  16.9 1.2 %ghost_fix.1 = (f32[3080,128]{1,0:T(8,128)S(1)}, f32[8192,128]{1,0:T(8,128)S(1)}, f32[1024,128]{1,0:T(8,128)S(1)}, f32[1024,128]{1,0:T(8,128)S(1)}) custom-call(s32[520]{0:T(1024)S(4)} %get-tuple-element.24.refs_0_, f32[512,128]{1,0:T(8,128)S(1)} %collective-permute-done.refs_1_, ...), custom_call_target="tpu_custom_call", output_to_operand_aliasing={{0}: (5, {}), {1}: (6, {}), {2}: (7, {}), {3}: (8, {})} | custom-call | bytes 3145728 | tf_op jit(solution)/shard_map/ghost_fix/pallas_call | solution.py:471
  18.1 1.1 %collective-permute-start.2 = (f32[1024,128]{1,0:T(8,128)S(1)}, f32[1024,128]{1,0:T(8,128)S(1)}, u32[]{:S(2)}, u32[]{:S(2)}) collective-permute-start(f32[1024,128]{1,0:T(8,128)S(1)} %get-tuple-element.31), channel_id=1, source_target_pairs={{0,16},{16,0},{1,17},{17,1},{2,18},{18,2},{3,19},{19,3},{4,20},{20... | collective-permute-start | bytes 1572872 | tf_op jit(solution)/shard_map/ppermute | solution.py:487
  19.2 2.0 %write_cells.1 = f32[8192,128]{1,0:T(8,128)} custom-call(f32[8192,128]{1,0:T(8,128)S(1)} %get-tuple-element.29.new), custom_call_target="tpu_custom_call" | custom-call | bytes 4194304 | tf_op jit(solution)/shard_map/write_cells/pallas_call | solution.py:489
  21.2 0.0 collective-permute-done.2.partner
  21.2 0.9 %level_gap.1 = f32[1024,128]{1,0:T(8,128)} custom-call(f32[1024,128]{1,0:T(8,128)S(1)} %get-tuple-element.30.keep, f32[1024,128]{1,0:T(8,128)S(1)} %collective-permute-done.2.partner), custom_call_target="tpu_custom_call" | custom-call | bytes 1048576 | tf_op jit(solution)/shard_map/level_gap/pallas_call | solution.py:500
  (1 shorter events, 0.0 us)
Async XLA Ops:
  4.0 12.9 %collective-permute-start.1 = (f32[512,128]{1,0:T(8,128)S(1)}, f32[512,128]{1,0:T(8,128)S(1)}, u32[]{:S(2)}, u32[]{:S(2)}) collective-permute-start(f32[512,128]{1,0:T(8,128)S(1)} %get-tuple-element.25), channel_id=1, source_target_pairs={{0,2},{2,0},{4,6},{6,4},{8,10},{10,8},{12,14},{14,12},{1,3},{3,1},... | collective-permute-start | bytes 786440 | tf_op jit(solution)/shard_map/ppermute | solution.py:440
  4.3 12.6 %collective-permute-start = (f32[512,128]{1,0:T(8,128)S(1)}, f32[512,128]{1,0:T(8,128)S(1)}, u32[]{:S(2)}, u32[]{:S(2)}) collective-permute-start(f32[512,128]{1,0:T(8,128)S(1)} %get-tuple-element.25), channel_id=1, source_target_pairs={{2,4},{6,8},{10,12},{4,2},{8,6},{12,10},{3,5},{7,9},{11,13},{5,3},... | collective-permute-start | bytes 786440 | tf_op jit(solution)/shard_map/ppermute | solution.py:441
  18.1 3.1 %collective-permute-start.2 = (f32[1024,128]{1,0:T(8,128)S(1)}, f32[1024,128]{1,0:T(8,128)S(1)}, u32[]{:S(2)}, u32[]{:S(2)}) collective-permute-start(f32[1024,128]{1,0:T(8,128)S(1)} %get-tuple-element.31), channel_id=1, source_target_pairs={{0,16},{16,0},{1,17},{17,1},{2,18},{18,2},{3,19},{19,3},{4,20},{20... | collective-permute-start | bytes 1572872 | tf_op jit(solution)/shard_map/ppermute | solution.py:487

commit v3 on v2

--- a/solution.py
+++ b/solution.py
@@ -82,7 +82,10 @@
         src = jnp.where(rev == 1, behind, ahead)
         p = lane + b * LANES
         fine = src + (p << 10) + (rev << 20) + jnp.where(src >= pipes, MARK, 0)
-        fed = jnp.maximum(ahead, behind) >= pipes
+        revs = [back[g * blocks + b : g * blocks + b + 1, :] for g in range(GROUPS)]
+        most = jnp.maximum(jnp.maximum(revs[0], revs[1]), jnp.maximum(revs[2], revs[3]))
+        least = jnp.minimum(jnp.minimum(revs[0], revs[1]), jnp.minimum(revs[2], revs[3]))
+        fed = jnp.maximum(ahead * (1 - least), behind * most) >= pipes
         coarse = ahead + (behind << 10) + (p << 20) + jnp.where(fed, MARK, 0)
         words[b : b + 1, :] = jnp.where(level == 0, fine, coarse)
     backf = back.astype(jnp.float32)
@@ -144,11 +147,11 @@
 
     @pl.loop(0, faces.shape[0] // 8)
     def _(m):
+        moved = [
+            outflow[pl.ds(pl.multiple_of(face_s[m * 8 + u] * 4, 4), 4), :] for u in range(8)
+        ]
         for u in range(8):
-            pipe = face_s[m * 8 + u]
-            face_rows[pl.ds(pl.multiple_of(m * 32, 32) + 4 * u, 4), :] = outflow[
-                pl.ds(pl.multiple_of(pipe * 4, 4), 4), :
-            ]
+            face_rows[pl.ds(pl.multiple_of(m * 32, 32) + 4 * u, 4), :] = moved[u]
 
 
 def eight_words(q, words):
@@ -176,11 +179,11 @@
     return count
 
 
-def fine_block(q, cells, rates, factor, boosts, flow_back, ahead_in, new, keep, send):
+def fine_block(q, cells, rates, factor, boosts, flow_back, ahead_in, new, shares):
+    kept, kept_mid, sent_mid, sent = shares
     own = pl.ds(pl.multiple_of(q * 8, 8), 8)
     base = pl.multiple_of(q * 128, 128)
     quad = pl.multiple_of(q * 32, 32)
-    pair = pl.multiple_of(q * 16, 16)
     rev = flow_back[own, :] != 0.0
     f = factor[own, :]
     b = f * rates[pl.ds(quad, 8, stride=4), :]
@@ -194,19 +197,18 @@
     y = [jnp.where(rev, o[SEGF - 1 - k], o[k]) for k in range(SEGF)]
     for k in range(SEGF):
         new[pl.ds(base + k, 8, stride=16), :] = y[k]
-    for k in range(SEGC):
-        share = ((y[4 * k] + y[4 * k + 1]) + (y[4 * k + 2] + y[4 * k + 3])) * 0.25
-        (keep if k < 2 else send)[pl.ds(pair + k % 2, 8, stride=2), :] = share
+    for k, dest in enumerate((kept, kept_mid, sent_mid, sent)):
+        dest[own, :] = ((y[4 * k] + y[4 * k + 1]) + (y[4 * k + 2] + y[4 * k + 3])) * 0.25
 
 
 def coarse_block(
-    q, cells, rates, factor, boosts, flow_back, ahead_in, behind_in, new, keep, send
+    q, cells, rates, factor, boosts, flow_back, ahead_in, behind_in, new, shares
 ):
+    kept, kept_mid, sent_mid, sent = shares
     pipes = factor.shape[0]
     own = pl.ds(pl.multiple_of(q * 8, 8), 8)
     base = pl.multiple_of(q * 128, 128)
     quad = pl.multiple_of(q * 32, 32)
-    pair = pl.multiple_of(q * 16, 16)
     f = factor[own, :]
     bo = boosts[own, :]
     for g in range(GROUPS):
@@ -226,32 +228,46 @@
         for k in range(SEGC):
             new[pl.ds(base + 4 * g + k, 8, stride=16), :] = y[k]
             if g == 0:
-                (send if k < 2 else keep)[pl.ds(pair + k % 2, 8, stride=2), :] = y[k]
+                (sent, sent_mid, kept_mid, kept)[k][own, :] = y[k]
 
 
 def step_kernel(
     words, cells, rates, outflow, factor, boosts, flow_back,
-    new, keep, send, ghosts, ahead_in, behind_in,
+    new, out, kept, kept_mid, sent_mid, sent, ghosts, ahead_in, behind_in, sems,
 ):
+    shares = (kept, kept_mid, sent_mid, sent)
     level = lax.axis_index("level")
     eights = factor.shape[0] // 8
+    parts = sems.shape[0]
+    rows = new.shape[0] // parts
+
+    def written(n):
+        part = pl.ds(pl.multiple_of(n * rows, rows), rows)
+        return pltpu.make_async_copy(new.at[part], out.at[part], sems.at[n])
 
     def run(fine):
         gather_eight(fine, 0, words, outflow, ahead_in, behind_in)
 
         def some(q, count):
             if fine:
-                fine_block(q, cells, rates, factor, boosts, flow_back, ahead_in, new, keep, send)
+                fine_block(q, cells, rates, factor, boosts, flow_back, ahead_in, new, shares)
             else:
                 coarse_block(
                     q, cells, rates, factor, boosts, flow_back, ahead_in, behind_in,
-                    new, keep, send,
+                    new, shares,
                 )
             later = jnp.minimum(q + 1, eights - 1)
             gather_eight(fine, later, words, outflow, ahead_in, behind_in)
             return list_eight(q, words, ghosts, count)
 
-        ghosts[8 * eights] = lax.fori_loop(0, eights, some, jnp.int32(0))
+        per = eights // parts
+
+        def part(n, count):
+            count = lax.fori_loop(n * per, (n + 1) * per, some, count)
+            written(n).start()
+            return count
+
+        ghosts[8 * eights] = lax.fori_loop(0, parts, part, jnp.int32(0))
 
     @pl.when(level == 0)
     def _():
@@ -260,6 +276,9 @@
     @pl.when(level == 1)
     def _():
         run(False)
+
+    for n in range(parts):
+        written(n).wait()
 
 
 def arrive_kernel(first, near, arrived, outflow_in, outflow):
@@ -270,20 +289,67 @@
     outflow[pl.ds(start, half), :] = arrived[...]
 
 
-def fine_fix(first, words, rates, factor, outflow, new, keep, send):
+def over_list(count, ghosts, width, each):
+    whole = count // width
+
+    @pl.loop(0, whole)
+    def _(m):
+        each([ghosts[m * width + u] for u in range(width)])
+
+    @pl.loop(whole * width, count)
+    def _(i):
+        each([ghosts[i]])
+
+
+def send_kernel(
+    first, ghosts, arrived, rates, factor, flow_back,
+    outflow_in, sent_in, new_in, kept_in, outflow, sent, new, kept,
+):
+    pipes = factor.shape[0]
+    level = lax.axis_index("level")
+    arrive_kernel(first, False, arrived, outflow_in, outflow)
+
+    def fine(entries):
+        done = []
+        for w in entries:
+            src, p, rev = w & 1023, w >> 10 & 1023, w >> 20 & 1
+            own = pl.ds(p, 1)
+            rows = outflow[pl.ds(pl.multiple_of(src * 4, 4), 4), :]
+            f, r = factor[own, :], rates[pl.ds(p * 4, 1), :]
+            total = rows[0:1]
+            for s in range(1, GROUPS):
+                total = f * total + rows[s : s + 1]
+            back = jnp.where(rev == 1, jnp.float32(0.25), jnp.float32(0.0))
+            done.append((own, sent[own, :] + f * r * total * back))
+        for own, row in done:
+            sent[own, :] = row
+
+    def coarse(entries):
+        coarse_fix(entries, rates, factor, flow_back, outflow, new, kept, sent)
+
+    @pl.when(level == 0)
+    def _():
+        over_list(ghosts[pipes], ghosts, 8, fine)
+
+    @pl.when(level == 1)
+    def _():
+        over_list(ghosts[pipes], ghosts, 4, coarse)
+
+
+def fine_fix(entries, rates, factor, outflow, new, kept):
     row = lax.broadcasted_iota(jnp.int32, (8, LANES), 0)
     loaded = []
-    for w in words:
+    for w in entries:
         src, p, rev = w & 1023, w >> 10 & 1023, w >> 20 & 1
         near = pl.ds(pl.multiple_of(p * 16 + 8 * rev, 8), 8)
-        kept, sent = pl.ds(p * 2, 1), pl.ds(p * 2 + 1, 1)
+        own = pl.ds(p, 1)
         inflow = [spread(outflow, src * 4 + s) for s in range(GROUPS)]
         loaded.append((
-            rev, near, kept, sent, spread(factor, p), spread(rates, p * 4), inflow,
-            new[near, :], keep[kept, :], send[sent, :],
+            rev, near, own, spread(factor, p), spread(rates, p * 4), inflow,
+            new[near, :], kept[own, :],
         ))
     done = []
-    for rev, near, kept, sent, f, r, inflow, tile, keep_row, send_row in loaded:
+    for rev, near, own, f, r, inflow, tile, kept_row in loaded:
         b = f * r
         a = f - b
         edge = row == 7 * rev
@@ -294,23 +360,18 @@
             up = jnp.where(edge, inflow[s], pltpu.roll(delta, shift, 0))
             delta = a * delta + b * up
             total = f * total + b * inflow[s]
-        part = total[0:1] * 0.25
-        back = jnp.where(rev == 1, jnp.float32(1.0), jnp.float32(0.0))
-        done.append((
-            near, kept, sent, tile + delta,
-            keep_row + part * (1.0 - back), send_row + part * back,
-        ))
-    for near, kept, sent, tile, keep_row, send_row in done:
+        ahead = jnp.where(rev == 1, jnp.float32(0.0), jnp.float32(0.25))
+        done.append((near, own, tile + delta, kept_row + total[0:1] * ahead))
+    for near, own, tile, kept_row in done:
         new[near, :] = tile
-        keep[kept, :] = keep_row
-        send[sent, :] = send_row
-
-
-def coarse_fix(first, words, rates, factor, flow_back, outflow, new, keep, send):
+        kept[own, :] = kept_row
+
+
+def coarse_fix(entries, rates, factor, flow_back, outflow, new, kept, sent):
     pipes = factor.shape[0]
     zeros = outflow.shape[0] - 8
     loaded = []
-    for w in words:
+    for w in entries:
         p = w >> 20 & 1023
         rows = []
         for src in (w & 1023, w >> 10 & 1023):
@@ -334,57 +395,64 @@
     for p, low, high, first_rows, last_rows in done:
         new[low, :] = first_rows
         new[high, :] = last_rows
-        send[pl.ds(p * 2, 1), :] = first_rows[0:1]
-        keep[pl.ds(p * 2 + 1, 1), :] = last_rows[0:1]
+        kept[pl.ds(p, 1), :] = last_rows[0:1]
+        sent[pl.ds(p, 1), :] = first_rows[0:1]
 
 
 def fix_kernel(
-    first, ghosts, arrived, rates, factor, flow_back,
-    outflow_in, new_in, keep_in, send_in, outflow, new, keep, send,
+    ghosts, rates, factor, outflow, new_in, kept_in, out_in, new, kept, out, sem
 ):
+    pipes = factor.shape[0]
     level = lax.axis_index("level")
-    arrive_kernel(first, False, arrived, outflow_in, outflow)
-    count = ghosts[factor.shape[0]]
-
-    def run(fix, *state):
-        def some(start, width):
-            at = [start + u for u in range(width)]
-            fix(first, [ghosts[i] for i in at], *state)
-
-        whole = count // 4
-
-        @pl.loop(0, whole)
-        def _(m):
-            some(m * 4, 4)
-
-        @pl.loop(whole * 4, count)
-        def _(i):
-            some(i, 1)
+    shift = jnp.where(level == 0, 10, 20)
+    count = ghosts[pipes]
+
+    def write(entries):
+        for w in entries:
+            p = lax.shift_right_logical(w, shift) & 1023
+            part = pl.ds(pl.multiple_of(p * SEGF, SEGF), SEGF)
+            pltpu.make_async_copy(new.at[part], out.at[part], sem).start()
+
+    def fine(entries):
+        fine_fix(entries, rates, factor, outflow, new, kept)
+        write(entries)
 
     @pl.when(level == 0)
     def _():
-        run(fine_fix, rates, factor, outflow, new, keep, send)
+        over_list(count, ghosts, 4, fine)
 
     @pl.when(level == 1)
     def _():
-        run(coarse_fix, rates, factor, flow_back, outflow, new, keep, send)
-
-
-def write_kernel(new, out, sems):
-    rows = new.shape[0] // sems.shape[0]
-    copies = []
-    for n in range(sems.shape[0]):
-        part = pl.ds(n * rows, rows)
-        copies.append(pltpu.make_async_copy(new.at[part], out.at[part], sems.at[n]))
-    for copy in copies:
-        copy.start()
-    for copy in copies:
-        copy.wait()
-
-
-def gap_kernel(keep, partner, gap):
-    sign = jnp.where(lax.axis_index("level") == 0, jnp.float32(1.0), jnp.float32(-1.0))
-    gap[...] = (keep[...] - partner[...]) * sign
+        over_list(count, ghosts, 8, write)
+
+    def wait(some):
+        part = pl.ds(0, SEGF * some)
+        pltpu.make_async_copy(new.at[part], out.at[part], sem).wait()
+
+    whole = count // 8
+
+    @pl.loop(0, whole)
+    def _(m):
+        wait(8)
+
+    @pl.loop(whole * 8, count)
+    def _(i):
+        wait(1)
+
+
+def gap_kernel(kept, kept_mid, partner_mid, partner, gap):
+    level = lax.axis_index("level")
+    sign = jnp.where(level == 0, jnp.float32(1.0), jnp.float32(-1.0))
+
+    @pl.loop(0, kept.shape[0] // 32)
+    def _(m):
+        for u in range(4):
+            own = pl.ds(pl.multiple_of(m * 32 + 8 * u, 8), 8)
+            pair = pl.multiple_of(m * 64 + 16 * u, 16)
+            gap[pl.ds(pair + level, 8, stride=2), :] = (kept[own, :] - partner[own, :]) * sign
+            gap[pl.ds(pair + 1 - level, 8, stride=2), :] = (
+                kept_mid[own, :] - partner_mid[own, :]
+            ) * sign
 
 
 def per_device(panels, courant, direction, decay, booster, feeder, face_index):
@@ -440,22 +508,25 @@
     near_rows = lax.ppermute(face_rows, "dom", near_pairs)
     far_rows = lax.ppermute(face_rows, "dom", far_pairs)
 
-    new, keep, send, ghosts = pl.pallas_call(
+    new, out, kept, kept_mid, sent_mid, sent, ghosts = pl.pallas_call(
         step_kernel,
         name="advance_step",
         in_specs=[SMEM] + [VMEM] * 6,
-        out_specs=[VMEM, VMEM, VMEM, SMEM],
+        out_specs=[VMEM, HBM] + [VMEM] * 4 + [SMEM],
         out_shape=[
             pltpu.VMEM((pipes * SEGF, columns), f32),
-            pltpu.VMEM((pipes * 2, columns), f32),
-            pltpu.VMEM((pipes * 2, columns), f32),
+            jax.ShapeDtypeStruct((pipes * SEGF, columns), f32),
+            *[pltpu.VMEM((pipes, columns), f32)] * 4,
             pltpu.SMEM((pipes + 8,), i32),
         ],
-        scratch_shapes=[pltpu.VMEM((GROUPS * pipes, columns), f32)] * 2,
+        scratch_shapes=[pltpu.VMEM((GROUPS * pipes, columns), f32)] * 2
+        + [pltpu.SemaphoreType.DMA((8,))],
         compiler_params=params(),
         cost_estimate=cost(20 << 20),
     )(words, cells, rates, outflow, factor, boosts, flow_back)
 
+    swap = [(0, 1), (1, 0)]
+    partner_mid = lax.ppermute(sent_mid, "level", swap)
     first = GROUPS * pipes
     outflow = pl.pallas_call(
         lambda *refs: arrive_kernel(first, True, *refs),
@@ -468,44 +539,49 @@
         cost_estimate=cost(1 << 19),
     )(near_rows, outflow)
 
-    outflow, new, keep, send = pl.pallas_call(
-        lambda *refs: fix_kernel(first, *refs),
-        name="ghost_fix",
+    outflow, sent, new, kept = pl.pallas_call(
+        lambda *refs: send_kernel(first, *refs),
+        name="ghost_send",
         in_specs=[SMEM] + [VMEM] * 8,
         out_specs=[VMEM] * 4,
         out_shape=[
             pltpu.VMEM((ghost_rows, columns), f32),
+            pltpu.VMEM((pipes, columns), f32),
             pltpu.VMEM((pipes * SEGF, columns), f32),
-            pltpu.VMEM((pipes * 2, columns), f32),
-            pltpu.VMEM((pipes * 2, columns), f32),
+            pltpu.VMEM((pipes, columns), f32),
         ],
         input_output_aliases={5: 0, 6: 1, 7: 2, 8: 3},
         compiler_params=params(),
-        cost_estimate=cost(3 << 20),
-    )(ghosts, far_rows, rates, factor, flow_back, outflow, new, keep, send)
-
-    partner = lax.ppermute(send, "level", [(0, 1), (1, 0)])
-
-    out = pl.pallas_call(
-        write_kernel,
-        name="write_cells",
-        in_specs=[VMEM],
-        out_specs=HBM,
-        out_shape=jax.ShapeDtypeStruct((pipes * SEGF, columns), f32),
-        scratch_shapes=[pltpu.SemaphoreType.DMA((4,))],
+        cost_estimate=cost(1 << 20),
+    )(ghosts, far_rows, rates, factor, flow_back, outflow, sent, new, kept)
+
+    partner = lax.ppermute(sent, "level", swap)
+
+    new, kept, out = pl.pallas_call(
+        fix_kernel,
+        name="ghost_fix",
+        in_specs=[SMEM] + [VMEM] * 5 + [HBM],
+        out_specs=[VMEM, VMEM, HBM],
+        out_shape=[
+            pltpu.VMEM((pipes * SEGF, columns), f32),
+            pltpu.VMEM((pipes, columns), f32),
+            jax.ShapeDtypeStruct((pipes * SEGF, columns), f32),
+        ],
+        scratch_shapes=[pltpu.SemaphoreType.DMA(())],
+        input_output_aliases={4: 0, 5: 1, 6: 2},
         compiler_params=params(),
         cost_estimate=cost(4 << 20),
-    )(new)
+    )(ghosts, rates, factor, outflow, new, kept, *pinned(pltpu.HBM, out))
 
     gap = pl.pallas_call(
         gap_kernel,
         name="level_gap",
-        in_specs=[VMEM] * 2,
+        in_specs=[VMEM] * 4,
         out_specs=VMEM,
         out_shape=jax.ShapeDtypeStruct((pipes * 2, columns), f32),
         compiler_params=params(),
         cost_estimate=cost(1 << 20),
-    )(keep, partner)
+    )(kept, kept_mid, partner_mid, partner)
     return (out.reshape(1, pipes, SEGF, columns), gap.reshape(pipes, 2, columns))
 
 

time: 22.4 us -> 21.3 us (0.951)
  waiting for transfers between devices: 2.02 us -> 0.25 us
  starting transfers between devices: 5.5 us -> 6.41 us
  Pallas kernels: 13.9 us -> 13.5 us
    ppermute x1, waiting for transfers between devices: 2.02 us -> 0.01 us  [per_device(): near_rows = lax.ppermute(face_rows, 'dom', near_pairs)]
    pallas_call x3, Pallas kernels: 4.07 us -> 2.64 us  [the longest x1 0.97 us: per_device(): pl.pallas_call(gap_kernel, name='level_gap', in_specs=[VMEM] * 4, out_spe...]
    pallas_call x1, Pallas kernels: 6.44 us -> 7.63 us  [per_device(): pl.pallas_call(step_kernel, name='advance_step', in_specs=[SMEM] + [VMEM]...]
    ppermute x1 -> x2, starting transfers between devices: 1.06 us -> 1.97 us  [the longest x1 1.19 us: per_device(): partner = lax.ppermute(sent, 'level', swap)]
    ppermute x1 -> x2, waiting for transfers between devices: 0.01 us -> 0.25 us  [the longest x1 0.24 us: per_device(): partner = lax.ppermute(sent, 'level', swap)]
  transfers between devices with their start and end apart: 3 -> 4, of which waited for: 1 -> 1; matrix products, arithmetic and copies ran while one was open for 0% -> 0% of each run, Pallas kernels for 38% -> 45%
where the time goes in v3:
time: 21.3 us; the launch traced here: 20.9 us
  Pallas kernels  13.5 us (63%)
  starting transfers between devices  6.41 us (30%)
  between operations  0.7 us (3%)
  waiting for transfers between devices  0.25 us (1%)
    pallas_call x1, Pallas kernels, per_device(): pl.pallas_call(step_kernel, name='advance_step', in_specs=[SMEM] + [VMEM]...  7.63 us
    ppermute x1, starting transfers between devices, per_device(): far_rows = lax.ppermute(face_rows, 'dom', far_pairs)  4.12 us
    pallas_call x1, Pallas kernels, per_device(): pl.pallas_call(load_kernel, name='load_step', in_specs=[HBM] * 7, out_spe...  3.21 us
    ppermute x1, starting transfers between devices, per_device(): partner = lax.ppermute(sent, 'level', swap)  1.19 us
    pallas_call x1, Pallas kernels, per_device(): pl.pallas_call(gap_kernel, name='level_gap', in_specs=[VMEM] * 4, out_spe...  0.97 us
    pallas_call x1, Pallas kernels, per_device(): pl.pallas_call(fix_kernel, name='ghost_fix', in_specs=[SMEM] + [VMEM] * 5...  0.9 us
    ppermute x1, starting transfers between devices, per_device(): partner_mid = lax.ppermute(sent_mid, 'level', swap)  0.78 us
    pallas_call x1, Pallas kernels, per_device(): pl.pallas_call(lambda *refs: send_kernel(first, *refs), name='ghost_send'...  0.77 us
  transfers between devices with their start and end apart: 4, of which 1 were waited for; matrix products, arithmetic and copies ran while one was open for 0% of the time, Pallas kernels for 45%

profile of v3, /device:TPU:11, one launch (start us, length us, event | category | flops | bytes accessed | tf_op | source)
XLA Modules:
  0.0 20.9 jit_solution(14629523369504652215)
XLA Ops:
  0.6 3.2 %load_step.1 = (f32[8192,128]{1,0:T(8,128)S(1)}, f32[2048,128]{1,0:T(8,128)S(1)}, f32[3080,128]{1,0:T(8,128)S(1)}, f32[512,128]{1,0:T(8,128)S(1)}, f32[512,128]{...) custom-call(f32[8192,128]{1,0:T(8,128)} %bitcast.14, ...), custom_call_target="tpu_custom_call" | custom-call | bytes 5242880 | tf_op jit(solution)/shard_map/load_step/pallas_call | solution.py:471
  3.8 0.3 %collective-permute-start.1 = (f32[512,128]{1,0:T(8,128)S(1)}, f32[512,128]{1,0:T(8,128)S(1)}, u32[]{:S(2)}, u32[]{:S(2)}) collective-permute-start(f32[512,128]{1,0:T(8,128)S(1)} %get-tuple-element.31), channel_id=1, source_target_pairs={{0,2},{2,0},{4,6},{6,4},{8,10},{10,8},{12,14},{14,12},{1,3},{3,1},... | collective-permute-start | bytes 786440 | tf_op jit(solution)/shard_map/ppermute | solution.py:508
  4.2 4.1 %collective-permute-start = (f32[512,128]{1,0:T(8,128)S(1)}, f32[512,128]{1,0:T(8,128)S(1)}, u32[]{:S(2)}, u32[]{:S(2)}) collective-permute-start(f32[512,128]{1,0:T(8,128)S(1)} %get-tuple-element.31), channel_id=1, source_target_pairs={{2,4},{6,8},{10,12},{4,2},{8,6},{12,10},{3,5},{7,9},{11,13},{5,3},... | collective-permute-start | bytes 786440 | tf_op jit(solution)/shard_map/ppermute | solution.py:509
  8.3 7.6 %advance_step.1 = (f32[8192,128]{1,0:T(8,128)S(1)}, f32[8192,128]{1,0:T(8,128)}, f32[512,128]{1,0:T(8,128)S(1)}, f32[512,128]{1,0:T(8,128)S(1)}, f32[512,128]{1,...) custom-call(s32[4,128]{1,0:T(4,128)S(1)} %get-tuple-element.23.words, f32[8192,128]{1,0:T(8,128)S(1)} %get-tuple-element.24.cells, ...), custom_call_target="tpu_custom_call" | custom-call | bytes 20971520 | tf_op jit(solution)/shard_map/advance_step/pallas_call | solution.py:511
  15.9 0.8 %collective-permute-start.2 = (f32[512,128]{1,0:T(8,128)S(1)}, f32[512,128]{1,0:T(8,128)S(1)}, u32[]{:S(2)}, u32[]{:S(2)}) collective-permute-start(f32[512,128]{1,0:T(8,128)S(1)} %get-tuple-element.42), channel_id=1, source_target_pairs={{0,16},{16,0},{1,17},{17,1},{2,18},{18,2},{3,19},{19,3},{4,20},{20... | collective-permute-start | bytes 786440 | tf_op jit(solution)/shard_map/ppermute | solution.py:529
  16.7 0.0 collective-permute-done.1.refs_0_
  16.8 0.0 collective-permute-done.refs_1_
  16.8 0.8 %ghost_send.1 = (f32[3080,128]{1,0:T(8,128)S(1)}, f32[512,128]{1,0:T(8,128)S(1)}, f32[8192,128]{1,0:T(8,128)S(1)}, f32[512,128]{1,0:T(8,128)S(1)}) custom-call(s32[520]{0:T(1024)S(4)} %get-tuple-element.30.refs_0_.ghosts, f32[512,128]{1,0:T(8,128)S(1)} %collective-permute-done.refs_1_, ...), custom_call_target="tpu_custom_call", output_to_operand_aliasing={{0}: (5, {}), {1}: (6, {}), {2}: (7, {}), {3}: (8, {})} | custom-call | bytes 1048576 | tf_op jit(solution)/shard_map/ghost_send/pallas_call | solution.py:542
  17.5 1.2 %collective-permute-start.3 = (f32[512,128]{1,0:T(8,128)S(1)}, f32[512,128]{1,0:T(8,128)S(1)}, u32[]{:S(2)}, u32[]{:S(2)}) collective-permute-start(f32[512,128]{1,0:T(8,128)S(1)} %get-tuple-element.43), channel_id=1, source_target_pairs={{0,16},{16,0},{1,17},{17,1},{2,18},{18,2},{3,19},{19,3},{4,20},{20... | collective-permute-start | bytes 786440 | tf_op jit(solution)/shard_map/ppermute | solution.py:558
  18.7 0.9 %ghost_fix.1 = (f32[8192,128]{1,0:T(8,128)S(1)}, f32[512,128]{1,0:T(8,128)S(1)}, f32[8192,128]{1,0:T(8,128)}) custom-call(s32[520]{0:T(1024)S(4)} %get-tuple-element.30.refs_0_.ghosts, f32[2048,128]{1,0:T(8,128)S(1)} %get-tuple-element.25.rates.refs_2_, ...), custom_call_target="tpu_custom_call", output_to_operand_aliasing={{0}: (4, {}), {1}: (5, {}), {2}: (6, {})} | custom-call | bytes 4194304 | tf_op jit(solution)/shard_map/ghost_fix/pallas_call | solution.py:560
  19.6 0.0 collective-permute-done.2.partner_mid
  19.7 0.2 %collective-permute-done.3.partner = f32[512,128]{1,0:T(8,128)S(1)} collective-permute-done((f32[512,128]{1,0:T(8,128)S(1)}, f32[512,128]{1,0:T(8,128)S(1)}, u32[]{:S(2)}, u32[]{:S(2)}) %collective-permute-start.3) | collective-permute-done | bytes 262176 | tf_op jit(solution)/shard_map/ppermute | solution.py:558
  19.9 1.0 %level_gap.1 = f32[1024,128]{1,0:T(8,128)} custom-call(f32[512,128]{1,0:T(8,128)S(1)} %get-tuple-element.40.kept, f32[512,128]{1,0:T(8,128)S(1)} %get-tuple-element.41.kept_mid, f32[512,128]{1,0:T(8,128)S(1)} %collective-permute-done.2.partner_mid, f32[512,128]{1,0:T(8,128)S(1)} %collective-permute-done.3.partner), custom_call_target="tpu_custom_call" | custom-call | bytes 1048576 | tf_op jit(solution)/shard_map/level_gap/pallas_call | solution.py:576
  (1 shorter events, 0.0 us)
Async XLA Ops:
  3.8 12.9 %collective-permute-start.1 = (f32[512,128]{1,0:T(8,128)S(1)}, f32[512,128]{1,0:T(8,128)S(1)}, u32[]{:S(2)}, u32[]{:S(2)}) collective-permute-start(f32[512,128]{1,0:T(8,128)S(1)} %get-tuple-element.31), channel_id=1, source_target_pairs={{0,2},{2,0},{4,6},{6,4},{8,10},{10,8},{12,14},{14,12},{1,3},{3,1},... | collective-permute-start | bytes 786440 | tf_op jit(solution)/shard_map/ppermute | solution.py:508
  4.2 12.6 %collective-permute-start = (f32[512,128]{1,0:T(8,128)S(1)}, f32[512,128]{1,0:T(8,128)S(1)}, u32[]{:S(2)}, u32[]{:S(2)}) collective-permute-start(f32[512,128]{1,0:T(8,128)S(1)} %get-tuple-element.31), channel_id=1, source_target_pairs={{2,4},{6,8},{10,12},{4,2},{8,6},{12,10},{3,5},{7,9},{11,13},{5,3},... | collective-permute-start | bytes 786440 | tf_op jit(solution)/shard_map/ppermute | solution.py:509
  15.9 3.7 %collective-permute-start.2 = (f32[512,128]{1,0:T(8,128)S(1)}, f32[512,128]{1,0:T(8,128)S(1)}, u32[]{:S(2)}, u32[]{:S(2)}) collective-permute-start(f32[512,128]{1,0:T(8,128)S(1)} %get-tuple-element.42), channel_id=1, source_target_pairs={{0,16},{16,0},{1,17},{17,1},{2,18},{18,2},{3,19},{19,3},{4,20},{20... | collective-permute-start | bytes 786440 | tf_op jit(solution)/shard_map/ppermute | solution.py:529
  17.5 2.4 %collective-permute-start.3 = (f32[512,128]{1,0:T(8,128)S(1)}, f32[512,128]{1,0:T(8,128)S(1)}, u32[]{:S(2)}, u32[]{:S(2)}) collective-permute-start(f32[512,128]{1,0:T(8,128)S(1)} %get-tuple-element.43), channel_id=1, source_target_pairs={{0,16},{16,0},{1,17},{17,1},{2,18},{18,2},{3,19},{19,3},{4,20},{20... | collective-permute-start | bytes 786440 | tf_op jit(solution)/shard_map/ppermute | solution.py:558

commit v4 on v3

--- a/solution.py
+++ b/solution.py
@@ -62,7 +62,7 @@
         copy.start()
     rate_copy.start()
     for n in range(CHUNKS):
-        chunk(n).start()
+        chunk(n).start(priority=1)
     for copy in small:
         copy.wait()
 
@@ -145,13 +145,13 @@
                         cells[pl.ds(base + 4 * g + 3, 8, stride=16), :],
                     )
 
-    @pl.loop(0, faces.shape[0] // 8)
+    @pl.loop(0, faces.shape[0] // 16)
     def _(m):
         moved = [
-            outflow[pl.ds(pl.multiple_of(face_s[m * 8 + u] * 4, 4), 4), :] for u in range(8)
+            outflow[pl.ds(pl.multiple_of(face_s[m * 16 + u] * 4, 4), 4), :] for u in range(16)
         ]
-        for u in range(8):
-            face_rows[pl.ds(pl.multiple_of(m * 32, 32) + 4 * u, 4), :] = moved[u]
+        for u in range(16):
+            face_rows[pl.ds(pl.multiple_of(m * 64, 64) + 4 * u, 4), :] = moved[u]
 
 
 def eight_words(q, words):
@@ -400,7 +400,8 @@
 
 
 def fix_kernel(
-    ghosts, rates, factor, outflow, new_in, kept_in, out_in, new, kept, out, sem
+    ghosts, rates, factor, outflow, kept_mid, partner_mid, new_in, kept_in, out_in,
+    new, kept, out, gap_rows, sem,
 ):
     pipes = factor.shape[0]
     level = lax.axis_index("level")
@@ -425,6 +426,15 @@
     def _():
         over_list(count, ghosts, 8, write)
 
+    sign = jnp.where(level == 0, jnp.float32(1.0), jnp.float32(-1.0))
+
+    @pl.loop(0, pipes // 64)
+    def _(m):
+        for u in range(8):
+            own = pl.ds(pl.multiple_of(m * 64 + 8 * u, 8), 8)
+            spots = pl.ds(pl.multiple_of(m * 128, 128) + 16 * u + 1 - level, 8, stride=2)
+            gap_rows[spots, :] = (kept_mid[own, :] - partner_mid[own, :]) * sign
+
     def wait(some):
         part = pl.ds(0, SEGF * some)
         pltpu.make_async_copy(new.at[part], out.at[part], sem).wait()
@@ -440,19 +450,21 @@
         wait(1)
 
 
-def gap_kernel(kept, kept_mid, partner_mid, partner, gap):
+def gap_kernel(kept, partner, rows_in, rows, gap, sems):
     level = lax.axis_index("level")
     sign = jnp.where(level == 0, jnp.float32(1.0), jnp.float32(-1.0))
-
-    @pl.loop(0, kept.shape[0] // 32)
-    def _(m):
-        for u in range(4):
-            own = pl.ds(pl.multiple_of(m * 32 + 8 * u, 8), 8)
-            pair = pl.multiple_of(m * 64 + 16 * u, 16)
-            gap[pl.ds(pair + level, 8, stride=2), :] = (kept[own, :] - partner[own, :]) * sign
-            gap[pl.ds(pair + 1 - level, 8, stride=2), :] = (
-                kept_mid[own, :] - partner_mid[own, :]
-            ) * sign
+    parts = sems.shape[0]
+    copies = []
+    per = kept.shape[0] // 8 // parts
+    for n in range(parts):
+        for q in range(n * per, (n + 1) * per):
+            own = pl.ds(8 * q, 8)
+            rows[pl.ds(16 * q + level, 8, stride=2), :] = (kept[own, :] - partner[own, :]) * sign
+        part = pl.ds(n * per * 16, per * 16)
+        copies.append(pltpu.make_async_copy(rows.at[part], gap.at[part], sems.at[n]))
+        copies[-1].start()
+    for copy in copies:
+        copy.wait()
 
 
 def per_device(panels, courant, direction, decay, booster, feeder, face_index):
@@ -557,31 +569,40 @@
 
     partner = lax.ppermute(sent, "level", swap)
 
-    new, kept, out = pl.pallas_call(
+    new, kept, out, gap_rows = pl.pallas_call(
         fix_kernel,
         name="ghost_fix",
-        in_specs=[SMEM] + [VMEM] * 5 + [HBM],
-        out_specs=[VMEM, VMEM, HBM],
+        in_specs=[SMEM] + [VMEM] * 7 + [HBM],
+        out_specs=[VMEM, VMEM, HBM, VMEM],
         out_shape=[
             pltpu.VMEM((pipes * SEGF, columns), f32),
             pltpu.VMEM((pipes, columns), f32),
             jax.ShapeDtypeStruct((pipes * SEGF, columns), f32),
+            pltpu.VMEM((pipes * 2, columns), f32),
         ],
         scratch_shapes=[pltpu.SemaphoreType.DMA(())],
-        input_output_aliases={4: 0, 5: 1, 6: 2},
+        input_output_aliases={6: 0, 7: 1, 8: 2},
         compiler_params=params(),
         cost_estimate=cost(4 << 20),
-    )(ghosts, rates, factor, outflow, new, kept, *pinned(pltpu.HBM, out))
-
-    gap = pl.pallas_call(
+    )(
+        ghosts, rates, factor, outflow, kept_mid, partner_mid, new, kept,
+        *pinned(pltpu.HBM, out),
+    )
+
+    _, gap = pl.pallas_call(
         gap_kernel,
         name="level_gap",
-        in_specs=[VMEM] * 4,
-        out_specs=VMEM,
-        out_shape=jax.ShapeDtypeStruct((pipes * 2, columns), f32),
+        in_specs=[VMEM] * 3,
+        out_specs=[VMEM, HBM],
+        out_shape=[
+            pltpu.VMEM((pipes * 2, columns), f32),
+            jax.ShapeDtypeStruct((pipes * 2, columns), f32),
+        ],
+        scratch_shapes=[pltpu.SemaphoreType.DMA((2,))],
+        input_output_aliases={2: 0},
         compiler_params=params(),
         cost_estimate=cost(1 << 20),
-    )(kept, kept_mid, partner_mid, partner)
+    )(kept, partner, gap_rows)
     return (out.reshape(1, pipes, SEGF, columns), gap.reshape(pipes, 2, columns))
 
 

time: 21.3 us -> 20.9 us (0.981)
  Pallas kernels: 13.5 us -> 13.1 us
    pallas_call x1, Pallas kernels: 3.21 us -> 2.98 us  [per_device(): pl.pallas_call(load_kernel, name='load_step', in_specs=[HBM] * 7, out_spe...]
where the time goes in v4:
time: 20.9 us; the launch traced here: 20.5 us
  Pallas kernels  13.1 us (63%)
  starting transfers between devices  6.42 us (31%)
  between operations  0.69 us (3%)
  waiting for transfers between devices  0.29 us (1%)
    pallas_call x1, Pallas kernels, per_device(): pl.pallas_call(step_kernel, name='advance_step', in_specs=[SMEM] + [VMEM]...  7.63 us
    ppermute x1, starting transfers between devices, per_device(): far_rows = lax.ppermute(face_rows, 'dom', far_pairs)  4.12 us
    pallas_call x1, Pallas kernels, per_device(): pl.pallas_call(load_kernel, name='load_step', in_specs=[HBM] * 7, out_spe...  2.98 us
    ppermute x1, starting transfers between devices, per_device(): partner = lax.ppermute(sent, 'level', swap)  1.24 us
    pallas_call x1, Pallas kernels, per_device(): pl.pallas_call(fix_kernel, name='ghost_fix', in_specs=[SMEM] + [VMEM] * 7...  0.89 us
    pallas_call x1, Pallas kernels, per_device(): pl.pallas_call(gap_kernel, name='level_gap', in_specs=[VMEM] * 3, out_spe...  0.83 us
    pallas_call x1, Pallas kernels, per_device(): pl.pallas_call(lambda *refs: send_kernel(first, *refs), name='ghost_send'...  0.76 us
    ppermute x1, starting transfers between devices, per_device(): partner_mid = lax.ppermute(sent_mid, 'level', swap)  0.74 us
  transfers between devices with their start and end apart: 4, of which 1 were waited for; matrix products, arithmetic and copies ran while one was open for 0% of the time, Pallas kernels for 45%

profile of v4, /device:TPU:11, one launch (start us, length us, event | category | flops | bytes accessed | tf_op | source)
XLA Modules:
  0.0 20.5 jit_solution(8294799905098791873)
XLA Ops:
  0.6 3.0 %load_step.1 = (f32[8192,128]{1,0:T(8,128)S(1)}, f32[2048,128]{1,0:T(8,128)S(1)}, f32[3080,128]{1,0:T(8,128)S(1)}, f32[512,128]{1,0:T(8,128)S(1)}, f32[512,128]{...) custom-call(f32[8192,128]{1,0:T(8,128)} %bitcast.14, ...), custom_call_target="tpu_custom_call" | custom-call | bytes 5242880 | tf_op jit(solution)/shard_map/load_step/pallas_call | solution.py:483
  3.6 0.3 %collective-permute-start.1 = (f32[512,128]{1,0:T(8,128)S(1)}, f32[512,128]{1,0:T(8,128)S(1)}, u32[]{:S(2)}, u32[]{:S(2)}) collective-permute-start(f32[512,128]{1,0:T(8,128)S(1)} %get-tuple-element.33), channel_id=1, source_target_pairs={{0,2},{2,0},{4,6},{6,4},{8,10},{10,8},{12,14},{14,12},{1,3},{3,1},... | collective-permute-start | bytes 786440 | tf_op jit(solution)/shard_map/ppermute | solution.py:520
  3.9 4.1 %collective-permute-start = (f32[512,128]{1,0:T(8,128)S(1)}, f32[512,128]{1,0:T(8,128)S(1)}, u32[]{:S(2)}, u32[]{:S(2)}) collective-permute-start(f32[512,128]{1,0:T(8,128)S(1)} %get-tuple-element.33), channel_id=1, source_target_pairs={{2,4},{6,8},{10,12},{4,2},{8,6},{12,10},{3,5},{7,9},{11,13},{5,3},... | collective-permute-start | bytes 786440 | tf_op jit(solution)/shard_map/ppermute | solution.py:521
  8.1 7.6 %advance_step.1 = (f32[8192,128]{1,0:T(8,128)S(1)}, f32[8192,128]{1,0:T(8,128)}, f32[512,128]{1,0:T(8,128)S(1)}, f32[512,128]{1,0:T(8,128)S(1)}, f32[512,128]{1,...) custom-call(s32[4,128]{1,0:T(4,128)S(1)} %get-tuple-element.25.words, f32[8192,128]{1,0:T(8,128)S(1)} %get-tuple-element.26.cells, ...), custom_call_target="tpu_custom_call" | custom-call | bytes 20971520 | tf_op jit(solution)/shard_map/advance_step/pallas_call | solution.py:523
  15.7 0.7 %collective-permute-start.2 = (f32[512,128]{1,0:T(8,128)S(1)}, f32[512,128]{1,0:T(8,128)S(1)}, u32[]{:S(2)}, u32[]{:S(2)}) collective-permute-start(f32[512,128]{1,0:T(8,128)S(1)} %get-tuple-element.39), channel_id=1, source_target_pairs={{0,16},{16,0},{1,17},{17,1},{2,18},{18,2},{3,19},{19,3},{4,20},{20... | collective-permute-start | bytes 786440 | tf_op jit(solution)/shard_map/ppermute | solution.py:541
  16.4 0.0 collective-permute-done.1.refs_0_
  16.5 0.0 collective-permute-done.refs_1_
  16.5 0.8 %ghost_send.1 = (f32[3080,128]{1,0:T(8,128)S(1)}, f32[512,128]{1,0:T(8,128)S(1)}, f32[8192,128]{1,0:T(8,128)S(1)}, f32[512,128]{1,0:T(8,128)S(1)}) custom-call(s32[520]{0:T(1024)S(4)} %get-tuple-element.32.refs_0_.ghosts, f32[512,128]{1,0:T(8,128)S(1)} %collective-permute-done.refs_1_, ...), custom_call_target="tpu_custom_call", output_to_operand_aliasing={{0}: (5, {}), {1}: (6, {}), {2}: (7, {}), {3}: (8, {})} | custom-call | bytes 1048576 | tf_op jit(solution)/shard_map/ghost_send/pallas_call | solution.py:554
  17.3 1.2 %collective-permute-start.3 = (f32[512,128]{1,0:T(8,128)S(1)}, f32[512,128]{1,0:T(8,128)S(1)}, u32[]{:S(2)}, u32[]{:S(2)}) collective-permute-start(f32[512,128]{1,0:T(8,128)S(1)} %get-tuple-element.45), channel_id=1, source_target_pairs={{0,16},{16,0},{1,17},{17,1},{2,18},{18,2},{3,19},{19,3},{4,20},{20... | collective-permute-start | bytes 786440 | tf_op jit(solution)/shard_map/ppermute | solution.py:570
  18.5 0.0 collective-permute-done.2.partner_mid
  18.5 0.9 %ghost_fix.1 = (f32[8192,128]{1,0:T(8,128)S(1)}, f32[512,128]{1,0:T(8,128)S(1)}, f32[8192,128]{1,0:T(8,128)}, f32[1024,128]{1,0:T(8,128)S(1)}) custom-call(s32[520]{0:T(1024)S(4)} %get-tuple-element.32.refs_0_.ghosts, f32[2048,128]{1,0:T(8,128)S(1)} %get-tuple-element.27.rates.refs_2_, ...), custom_call_target="tpu_custom_call", output_to_operand_aliasing={{0}: (6, {}), {1}: (7, {}), {2}: (8, {})} | custom-call | bytes 4194304 | tf_op jit(solution)/shard_map/ghost_fix/pallas_call | solution.py:572
  19.4 0.3 %collective-permute-done.3.partner = f32[512,128]{1,0:T(8,128)S(1)} collective-permute-done((f32[512,128]{1,0:T(8,128)S(1)}, f32[512,128]{1,0:T(8,128)S(1)}, u32[]{:S(2)}, u32[]{:S(2)}) %collective-permute-start.3) | collective-permute-done | bytes 262176 | tf_op jit(solution)/shard_map/ppermute | solution.py:570
  19.7 0.8 %level_gap.1 = (f32[1024,128]{1,0:T(8,128)S(1)}, f32[1024,128]{1,0:T(8,128)}) custom-call(f32[512,128]{1,0:T(8,128)S(1)} %get-tuple-element.44.kept, f32[512,128]{1,0:T(8,128)S(1)} %collective-permute-done.3.partner, f32[1024,128]{1,0:T(8,128)S(1)} %get-tuple-element.46.rows_in), custom_call_target="tpu_custom_call", output_to_operand_aliasing={{0}: (2, {})} | custom-call | bytes 1048576 | tf_op jit(solution)/shard_map/level_gap/pallas_call | solution.py:592
  (1 shorter events, 0.0 us)
Async XLA Ops:
  3.6 12.9 %collective-permute-start.1 = (f32[512,128]{1,0:T(8,128)S(1)}, f32[512,128]{1,0:T(8,128)S(1)}, u32[]{:S(2)}, u32[]{:S(2)}) collective-permute-start(f32[512,128]{1,0:T(8,128)S(1)} %get-tuple-element.33), channel_id=1, source_target_pairs={{0,2},{2,0},{4,6},{6,4},{8,10},{10,8},{12,14},{14,12},{1,3},{3,1},... | collective-permute-start | bytes 786440 | tf_op jit(solution)/shard_map/ppermute | solution.py:520
  3.9 12.6 %collective-permute-start = (f32[512,128]{1,0:T(8,128)S(1)}, f32[512,128]{1,0:T(8,128)S(1)}, u32[]{:S(2)}, u32[]{:S(2)}) collective-permute-start(f32[512,128]{1,0:T(8,128)S(1)} %get-tuple-element.33), channel_id=1, source_target_pairs={{2,4},{6,8},{10,12},{4,2},{8,6},{12,10},{3,5},{7,9},{11,13},{5,3},... | collective-permute-start | bytes 786440 | tf_op jit(solution)/shard_map/ppermute | solution.py:521
  15.7 2.8 %collective-permute-start.2 = (f32[512,128]{1,0:T(8,128)S(1)}, f32[512,128]{1,0:T(8,128)S(1)}, u32[]{:S(2)}, u32[]{:S(2)}) collective-permute-start(f32[512,128]{1,0:T(8,128)S(1)} %get-tuple-element.39), channel_id=1, source_target_pairs={{0,16},{16,0},{1,17},{17,1},{2,18},{18,2},{3,19},{19,3},{4,20},{20... | collective-permute-start | bytes 786440 | tf_op jit(solution)/shard_map/ppermute | solution.py:541
  17.3 2.4 %collective-permute-start.3 = (f32[512,128]{1,0:T(8,128)S(1)}, f32[512,128]{1,0:T(8,128)S(1)}, u32[]{:S(2)}, u32[]{:S(2)}) collective-permute-start(f32[512,128]{1,0:T(8,128)S(1)} %get-tuple-element.45), channel_id=1, source_target_pairs={{0,16},{16,0},{1,17},{17,1},{2,18},{18,2},{3,19},{19,3},{4,20},{20... | collective-permute-start | bytes 786440 | tf_op jit(solution)/shard_map/ppermute | solution.py:570

commit v5 on v4

--- a/solution.py
+++ b/solution.py
@@ -60,7 +60,11 @@
     rate_copy = pltpu.make_async_copy(rate, rates, rate_sem)
     for copy in small:
         copy.start()
-    rate_copy.start()
+
+    @pl.when(level == 0)
+    def _():
+        rate_copy.start()
+
     for n in range(CHUNKS):
         chunk(n).start(priority=1)
     for copy in small:
@@ -102,11 +106,12 @@
         for g in range(1, GROUPS):
             back_rows(g)
 
-    rate_copy.wait()
     per_chunk = pipes // 8 // CHUNKS
 
     @pl.when(level == 0)
     def _():
+        rate_copy.wait()
+
         @pl.loop(0, CHUNKS)
         def _(n):
             chunk(n).wait()
@@ -232,8 +237,9 @@
 
 
 def step_kernel(
-    words, cells, rates, outflow, factor, boosts, flow_back,
-    new, out, kept, kept_mid, sent_mid, sent, ghosts, ahead_in, behind_in, sems,
+    words, rate, cells, rates_in, outflow, factor, boosts, flow_back,
+    new, out, kept, kept_mid, sent_mid, sent, ghosts, rates,
+    ahead_in, behind_in, sems, rate_sems,
 ):
     shares = (kept, kept_mid, sent_mid, sent)
     level = lax.axis_index("level")
@@ -245,7 +251,16 @@
         part = pl.ds(pl.multiple_of(n * rows, rows), rows)
         return pltpu.make_async_copy(new.at[part], out.at[part], sems.at[n])
 
+    rate_rows = rates.shape[0] // parts
+
+    def fetched(n):
+        part = pl.ds(pl.multiple_of(n * rate_rows, rate_rows), rate_rows)
+        return pltpu.make_async_copy(rate.at[part], rates.at[part], rate_sems.at[n])
+
     def run(fine):
+        if not fine:
+            for n in range(parts):
+                fetched(n).start()
         gather_eight(fine, 0, words, outflow, ahead_in, behind_in)
 
         def some(q, count):
@@ -263,6 +278,8 @@
         per = eights // parts
 
         def part(n, count):
+            if not fine:
+                fetched(n).wait()
             count = lax.fori_loop(n * per, (n + 1) * per, some, count)
             written(n).start()
             return count
@@ -480,6 +497,10 @@
     feed = feeder.reshape(blocks, LANES, 2).transpose(0, 2, 1).reshape(2 * blocks, LANES)
     ghost_rows = GROUPS * (pipes + 2 * faces) + 8
 
+    cells_in, rates_in, dirs, feed, decay, booster, face_index = pinned(
+        pltpu.HBM, cells_in, rates_in, dirs, feed,
+        decay.reshape(blocks, LANES), booster.reshape(blocks, LANES), face_index,
+    )
     cells, rates, outflow, factor, boosts, flow_back, words, face_rows = pl.pallas_call(
         load_kernel,
         name="load_step",
@@ -507,12 +528,7 @@
         ],
         compiler_params=params(),
         cost_estimate=cost(5 << 20),
-    )(
-        *pinned(
-            pltpu.HBM, cells_in, rates_in, dirs, feed,
-            decay.reshape(blocks, LANES), booster.reshape(blocks, LANES), face_index,
-        )
-    )
+    )(cells_in, rates_in, dirs, feed, decay, booster, face_index)
 
     near_pairs = [(i, i ^ 1) for i in range(domains) if i ^ 1 < domains]
     far_pairs = [(i, i + 1) for i in range(1, domains - 1, 2)]
@@ -520,22 +536,24 @@
     near_rows = lax.ppermute(face_rows, "dom", near_pairs)
     far_rows = lax.ppermute(face_rows, "dom", far_pairs)
 
-    new, out, kept, kept_mid, sent_mid, sent, ghosts = pl.pallas_call(
+    new, out, kept, kept_mid, sent_mid, sent, ghosts, rates = pl.pallas_call(
         step_kernel,
         name="advance_step",
-        in_specs=[SMEM] + [VMEM] * 6,
-        out_specs=[VMEM, HBM] + [VMEM] * 4 + [SMEM],
+        in_specs=[SMEM, HBM] + [VMEM] * 6,
+        out_specs=[VMEM, HBM] + [VMEM] * 4 + [SMEM, VMEM],
         out_shape=[
             pltpu.VMEM((pipes * SEGF, columns), f32),
             jax.ShapeDtypeStruct((pipes * SEGF, columns), f32),
             *[pltpu.VMEM((pipes, columns), f32)] * 4,
             pltpu.SMEM((pipes + 8,), i32),
+            pltpu.VMEM((pipes * GROUPS, columns), f32),
         ],
         scratch_shapes=[pltpu.VMEM((GROUPS * pipes, columns), f32)] * 2
-        + [pltpu.SemaphoreType.DMA((8,))],
+        + [pltpu.SemaphoreType.DMA((8,))] * 2,
+        input_output_aliases={3: 7},
         compiler_params=params(),
         cost_estimate=cost(20 << 20),
-    )(words, cells, rates, outflow, factor, boosts, flow_back)
+    )(words, rates_in, cells, rates, outflow, factor, boosts, flow_back)
 
     swap = [(0, 1), (1, 0)]
     partner_mid = lax.ppermute(sent_mid, "level", swap)

time: 20.9 us -> 20.6 us (0.986)
  starting transfers between devices: 6.42 us -> 5.48 us
  Pallas kernels: 13.1 us -> 13.8 us
    pallas_call x1, Pallas kernels: 7.63 us -> 8.59 us  [per_device(): pl.pallas_call(step_kernel, name='advance_step', in_specs=[SMEM, HBM] + [...]
    ppermute x1, starting transfers between devices: 0.74 us -> 0.18 us  [per_device(): partner_mid = lax.ppermute(sent_mid, 'level', swap)]
    ppermute x1, starting transfers between devices: 1.24 us -> 0.86 us  [per_device(): partner = lax.ppermute(sent, 'level', swap)]
    pallas_call x1, Pallas kernels: 2.98 us -> 2.66 us  [per_device(): pl.pallas_call(load_kernel, name='load_step', in_specs=[HBM] * 7, out_spe...]
  transfers between devices with their start and end apart: 4 -> 4, of which waited for: 1 -> 1; matrix products, arithmetic and copies ran while one was open for 0% -> 0% of each run, Pallas kernels for 45% -> 51%
where the time goes in v5:
time: 20.6 us; the launch traced here: 20.2 us
  Pallas kernels  13.8 us (67%)
  starting transfers between devices  5.48 us (27%)
  between operations  0.69 us (3%)
  waiting for transfers between devices  0.26 us (1%)
    pallas_call x1, Pallas kernels, per_device(): pl.pallas_call(step_kernel, name='advance_step', in_specs=[SMEM, HBM] + [...  8.59 us
    ppermute x1, starting transfers between devices, per_device(): far_rows = lax.ppermute(face_rows, 'dom', far_pairs)  4.12 us
    pallas_call x1, Pallas kernels, per_device(): pl.pallas_call(load_kernel, name='load_step', in_specs=[HBM] * 7, out_spe...  2.66 us
    pallas_call x1, Pallas kernels, per_device(): pl.pallas_call(fix_kernel, name='ghost_fix', in_specs=[SMEM] + [VMEM] * 7...  0.9 us
    ppermute x1, starting transfers between devices, per_device(): partner = lax.ppermute(sent, 'level', swap)  0.86 us
    pallas_call x1, Pallas kernels, per_device(): pl.pallas_call(gap_kernel, name='level_gap', in_specs=[VMEM] * 3, out_spe...  0.83 us
    pallas_call x1, Pallas kernels, per_device(): pl.pallas_call(lambda *refs: send_kernel(first, *refs), name='ghost_send'...  0.77 us
  transfers between devices with their start and end apart: 4, of which 1 were waited for; matrix products, arithmetic and copies ran while one was open for 0% of the time, Pallas kernels for 51%

profile of v5, /device:TPU:11, one launch (start us, length us, event | category | flops | bytes accessed | tf_op | source)
XLA Modules:
  0.0 20.2 jit_solution(213932020996412888)
XLA Ops:
  0.6 2.7 %load_step.1 = (f32[8192,128]{1,0:T(8,128)S(1)}, f32[2048,128]{1,0:T(8,128)S(1)}, f32[3080,128]{1,0:T(8,128)S(1)}, f32[512,128]{1,0:T(8,128)S(1)}, f32[512,128]{...) custom-call(f32[8192,128]{1,0:T(8,128)} %bitcast.14, ...), custom_call_target="tpu_custom_call" | custom-call | bytes 5242880 | tf_op jit(solution)/shard_map/load_step/pallas_call | solution.py:504
  3.3 0.3 %collective-permute-start.1 = (f32[512,128]{1,0:T(8,128)S(1)}, f32[512,128]{1,0:T(8,128)S(1)}, u32[]{:S(2)}, u32[]{:S(2)}) collective-permute-start(f32[512,128]{1,0:T(8,128)S(1)} %get-tuple-element.35), channel_id=1, source_target_pairs={{0,2},{2,0},{4,6},{6,4},{8,10},{10,8},{12,14},{14,12},{1,3},{3,1},... | collective-permute-start | bytes 786440 | tf_op jit(solution)/shard_map/ppermute | solution.py:536
  3.6 4.1 %collective-permute-start = (f32[512,128]{1,0:T(8,128)S(1)}, f32[512,128]{1,0:T(8,128)S(1)}, u32[]{:S(2)}, u32[]{:S(2)}) collective-permute-start(f32[512,128]{1,0:T(8,128)S(1)} %get-tuple-element.35), channel_id=1, source_target_pairs={{2,4},{6,8},{10,12},{4,2},{8,6},{12,10},{3,5},{7,9},{11,13},{5,3},... | collective-permute-start | bytes 786440 | tf_op jit(solution)/shard_map/ppermute | solution.py:537
  7.7 8.6 %advance_step.1 = (f32[8192,128]{1,0:T(8,128)S(1)}, f32[8192,128]{1,0:T(8,128)}, f32[512,128]{1,0:T(8,128)S(1)}, f32[512,128]{1,0:T(8,128)S(1)}, f32[512,128]{1,...) custom-call(s32[4,128]{1,0:T(4,128)S(1)} %get-tuple-element.26.words, ...), custom_call_target="tpu_custom_call", output_to_operand_aliasing={{7}: (3, {})} | custom-call | bytes 20971520 | tf_op jit(solution)/shard_map/advance_step/pallas_call | solution.py:539
  16.3 0.2 collective-permute-start.2
  16.5 0.0 collective-permute-done.1.refs_0_
  16.6 0.0 collective-permute-done.refs_1_
  16.6 0.8 %ghost_send.1 = (f32[3080,128]{1,0:T(8,128)S(1)}, f32[512,128]{1,0:T(8,128)S(1)}, f32[8192,128]{1,0:T(8,128)S(1)}, f32[512,128]{1,0:T(8,128)S(1)}) custom-call(s32[520]{0:T(1024)S(4)} %get-tuple-element.33.refs_0_.ghosts, f32[512,128]{1,0:T(8,128)S(1)} %collective-permute-done.refs_1_, ...), custom_call_target="tpu_custom_call", output_to_operand_aliasing={{0}: (5, {}), {1}: (6, {}), {2}: (7, {}), {3}: (8, {})} | custom-call | bytes 1048576 | tf_op jit(solution)/shard_map/ghost_send/pallas_call | solution.py:572
  17.4 0.9 %collective-permute-start.3 = (f32[512,128]{1,0:T(8,128)S(1)}, f32[512,128]{1,0:T(8,128)S(1)}, u32[]{:S(2)}, u32[]{:S(2)}) collective-permute-start(f32[512,128]{1,0:T(8,128)S(1)} %get-tuple-element.47), channel_id=1, source_target_pairs={{0,16},{16,0},{1,17},{17,1},{2,18},{18,2},{3,19},{19,3},{4,20},{20... | collective-permute-start | bytes 786440 | tf_op jit(solution)/shard_map/ppermute | solution.py:588
  18.2 0.0 collective-permute-done.2.partner_mid
  18.2 0.9 %ghost_fix.1 = (f32[8192,128]{1,0:T(8,128)S(1)}, f32[512,128]{1,0:T(8,128)S(1)}, f32[8192,128]{1,0:T(8,128)}, f32[1024,128]{1,0:T(8,128)S(1)}) custom-call(s32[520]{0:T(1024)S(4)} %get-tuple-element.33.refs_0_.ghosts, f32[2048,128]{1,0:T(8,128)S(1)} %get-tuple-element.34.refs_2_.rates, ...), custom_call_target="tpu_custom_call", output_to_operand_aliasing={{0}: (6, {}), {1}: (7, {}), {2}: (8, {})} | custom-call | bytes 4194304 | tf_op jit(solution)/shard_map/ghost_fix/pallas_call | solution.py:590
  19.1 0.2 %collective-permute-done.3.partner = f32[512,128]{1,0:T(8,128)S(1)} collective-permute-done((f32[512,128]{1,0:T(8,128)S(1)}, f32[512,128]{1,0:T(8,128)S(1)}, u32[]{:S(2)}, u32[]{:S(2)}) %collective-permute-start.3) | collective-permute-done | bytes 262176 | tf_op jit(solution)/shard_map/ppermute | solution.py:588
  19.4 0.8 %level_gap.1 = (f32[1024,128]{1,0:T(8,128)S(1)}, f32[1024,128]{1,0:T(8,128)}) custom-call(f32[512,128]{1,0:T(8,128)S(1)} %get-tuple-element.46.kept, f32[512,128]{1,0:T(8,128)S(1)} %collective-permute-done.3.partner, f32[1024,128]{1,0:T(8,128)S(1)} %get-tuple-element.48.rows_in), custom_call_target="tpu_custom_call", output_to_operand_aliasing={{0}: (2, {})} | custom-call | bytes 1048576 | tf_op jit(solution)/shard_map/level_gap/pallas_call | solution.py:610
  (1 shorter events, 0.0 us)
Async XLA Ops:
  3.3 13.2 %collective-permute-start.1 = (f32[512,128]{1,0:T(8,128)S(1)}, f32[512,128]{1,0:T(8,128)S(1)}, u32[]{:S(2)}, u32[]{:S(2)}) collective-permute-start(f32[512,128]{1,0:T(8,128)S(1)} %get-tuple-element.35), channel_id=1, source_target_pairs={{0,2},{2,0},{4,6},{6,4},{8,10},{10,8},{12,14},{14,12},{1,3},{3,1},... | collective-permute-start | bytes 786440 | tf_op jit(solution)/shard_map/ppermute | solution.py:536
  3.6 12.9 %collective-permute-start = (f32[512,128]{1,0:T(8,128)S(1)}, f32[512,128]{1,0:T(8,128)S(1)}, u32[]{:S(2)}, u32[]{:S(2)}) collective-permute-start(f32[512,128]{1,0:T(8,128)S(1)} %get-tuple-element.35), channel_id=1, source_target_pairs={{2,4},{6,8},{10,12},{4,2},{8,6},{12,10},{3,5},{7,9},{11,13},{5,3},... | collective-permute-start | bytes 786440 | tf_op jit(solution)/shard_map/ppermute | solution.py:537
  16.3 1.9 %collective-permute-start.2 = (f32[512,128]{1,0:T(8,128)S(1)}, f32[512,128]{1,0:T(8,128)S(1)}, u32[]{:S(2)}, u32[]{:S(2)}) collective-permute-start(f32[512,128]{1,0:T(8,128)S(1)} %get-tuple-element.41), channel_id=1, source_target_pairs={{0,16},{16,0},{1,17},{17,1},{2,18},{18,2},{3,19},{19,3},{4,20},{20... | collective-permute-start | bytes 786440 | tf_op jit(solution)/shard_map/ppermute | solution.py:559
  17.4 2.0 %collective-permute-start.3 = (f32[512,128]{1,0:T(8,128)S(1)}, f32[512,128]{1,0:T(8,128)S(1)}, u32[]{:S(2)}, u32[]{:S(2)}) collective-permute-start(f32[512,128]{1,0:T(8,128)S(1)} %get-tuple-element.47), channel_id=1, source_target_pairs={{0,16},{16,0},{1,17},{17,1},{2,18},{18,2},{3,19},{19,3},{4,20},{20... | collective-permute-start | bytes 786440 | tf_op jit(solution)/shard_map/ppermute | solution.py:588

commit v6 on v5

--- a/solution.py
+++ b/solution.py
@@ -9,7 +9,7 @@
 SEGC = 4
 GROUPS = SEGF // SEGC
 LANES = 128
-CHUNKS = 4
+CHUNKS = 8
 MARK = -(1 << 31)
 
 HBM = pl.BlockSpec(memory_space=pltpu.HBM)
@@ -34,7 +34,7 @@
 
 
 def spread(ref, row):
-    return ref[pl.ds(row, 8, stride=0), :]
+    return jnp.broadcast_to(ref[pl.ds(row, 1), :], (8, LANES))
 
 
 def load_kernel(
@@ -281,7 +281,10 @@
             if not fine:
                 fetched(n).wait()
             count = lax.fori_loop(n * per, (n + 1) * per, some, count)
-            written(n).start()
+            @pl.when(n < parts - 1)
+            def _():
+                written(n).start()
+
             return count
 
         ghosts[8 * eights] = lax.fori_loop(0, parts, part, jnp.int32(0))
@@ -294,7 +297,7 @@
     def _():
         run(False)
 
-    for n in range(parts):
+    for n in range(parts - 1):
         written(n).wait()
 
 
@@ -398,7 +401,7 @@
         high = pl.ds(p * 16 + 3, 4, stride=4)
         loaded.append((
             p, low, high, rows, flow_back[pl.ds(p, 4, stride=pipes), :],
-            rates[pl.ds(pl.multiple_of(p * 4, 4), 4), :], factor[pl.ds(p, 4, stride=0), :],
+            rates[pl.ds(pl.multiple_of(p * 4, 4), 4), :], jnp.broadcast_to(factor[pl.ds(p, 1), :], (4, LANES)),
             new[low, :], new[high, :],
         ))
     done = []
@@ -418,7 +421,7 @@
 
 def fix_kernel(
     ghosts, rates, factor, outflow, kept_mid, partner_mid, new_in, kept_in, out_in,
-    new, kept, out, gap_rows, sem,
+    new, kept, out, gap_rows, sem, tail_sem,
 ):
     pipes = factor.shape[0]
     level = lax.axis_index("level")
@@ -443,6 +446,9 @@
     def _():
         over_list(count, ghosts, 8, write)
 
+    tail = pl.ds(pipes * SEGF // 8 * 7, pipes * SEGF // 8)
+    last = pltpu.make_async_copy(new.at[tail], out.at[tail], tail_sem)
+    last.start()
     sign = jnp.where(level == 0, jnp.float32(1.0), jnp.float32(-1.0))
 
     @pl.loop(0, pipes // 64)
@@ -465,6 +471,8 @@
     @pl.loop(whole * 8, count)
     def _(i):
         wait(1)
+
+    last.wait()
 
 
 def gap_kernel(kept, partner, rows_in, rows, gap, sems):
@@ -598,7 +606,7 @@
             jax.ShapeDtypeStruct((pipes * SEGF, columns), f32),
             pltpu.VMEM((pipes * 2, columns), f32),
         ],
-        scratch_shapes=[pltpu.SemaphoreType.DMA(())],
+        scratch_shapes=[pltpu.SemaphoreType.DMA(())] * 2,
         input_output_aliases={6: 0, 7: 1, 8: 2},
         compiler_params=params(),
         cost_estimate=cost(4 << 20),

time: 20.6 us -> 20.4 us (level)
  starting transfers between devices: 5.48 us -> 6.21 us
  Pallas kernels: 13.8 us -> 13.3 us
  waiting for transfers between devices: 0.26 us -> 0.02 us
    pallas_call x1, Pallas kernels: 8.59 us -> 7.82 us  [per_device(): pl.pallas_call(step_kernel, name='advance_step', in_specs=[SMEM, HBM] + [...]
    ppermute x1, starting transfers between devices: 0.86 us -> 1.52 us  [per_device(): partner = lax.ppermute(sent, 'level', swap)]
    pallas_call x1, Pallas kernels: 0.9 us -> 1.14 us  [per_device(): pl.pallas_call(fix_kernel, name='ghost_fix', in_specs=[SMEM] + [VMEM] * 7...]
    ppermute x1, waiting for transfers between devices: 0.25 us -> 0.01 us  [per_device(): partner = lax.ppermute(sent, 'level', swap)]
  transfers between devices with their start and end apart: 4 -> 4, of which waited for: 1 -> 0; matrix products, arithmetic and copies ran while one was open for 0% -> 0% of each run, Pallas kernels for 51% -> 49%
where the time goes in v6:
time: 20.4 us; the launch traced here: 20.2 us
  Pallas kernels  13.3 us (65%)
  starting transfers between devices  6.21 us (30%)
  between operations  0.69 us (3%)
    pallas_call x1, Pallas kernels, per_device(): pl.pallas_call(step_kernel, name='advance_step', in_specs=[SMEM, HBM] + [...  7.82 us
    ppermute x1, starting transfers between devices, per_device(): far_rows = lax.ppermute(face_rows, 'dom', far_pairs)  4.12 us
    pallas_call x1, Pallas kernels, per_device(): pl.pallas_call(load_kernel, name='load_step', in_specs=[HBM] * 7, out_spe...  2.58 us
    ppermute x1, starting transfers between devices, per_device(): partner = lax.ppermute(sent, 'level', swap)  1.52 us
    pallas_call x1, Pallas kernels, per_device(): pl.pallas_call(fix_kernel, name='ghost_fix', in_specs=[SMEM] + [VMEM] * 7...  1.14 us
    pallas_call x1, Pallas kernels, per_device(): pl.pallas_call(lambda *refs: send_kernel(first, *refs), name='ghost_send'...  0.87 us
    pallas_call x1, Pallas kernels, per_device(): pl.pallas_call(gap_kernel, name='level_gap', in_specs=[VMEM] * 3, out_spe...  0.83 us
  transfers between devices with their start and end apart: 4, of which 0 were waited for; matrix products, arithmetic and copies ran while one was open for 0% of the time, Pallas kernels for 49%

profile of v6, /device:TPU:11, one launch (start us, length us, event | category | flops | bytes accessed | tf_op | source)
XLA Modules:
  0.0 20.2 jit_solution(13767573037416920339)
XLA Ops:
  0.6 2.6 %load_step.1 = (f32[8192,128]{1,0:T(8,128)S(1)}, f32[2048,128]{1,0:T(8,128)S(1)}, f32[3080,128]{1,0:T(8,128)S(1)}, f32[512,128]{1,0:T(8,128)S(1)}, f32[512,128]{...) custom-call(f32[8192,128]{1,0:T(8,128)} %bitcast.14, ...), custom_call_target="tpu_custom_call" | custom-call | bytes 5242880 | tf_op jit(solution)/shard_map/load_step/pallas_call | solution.py:512
  3.2 0.3 %collective-permute-start.1 = (f32[512,128]{1,0:T(8,128)S(1)}, f32[512,128]{1,0:T(8,128)S(1)}, u32[]{:S(2)}, u32[]{:S(2)}) collective-permute-start(f32[512,128]{1,0:T(8,128)S(1)} %get-tuple-element.35), channel_id=1, source_target_pairs={{0,2},{2,0},{4,6},{6,4},{8,10},{10,8},{12,14},{14,12},{1,3},{3,1},... | collective-permute-start | bytes 786440 | tf_op jit(solution)/shard_map/ppermute | solution.py:544
  3.5 4.1 %collective-permute-start = (f32[512,128]{1,0:T(8,128)S(1)}, f32[512,128]{1,0:T(8,128)S(1)}, u32[]{:S(2)}, u32[]{:S(2)}) collective-permute-start(f32[512,128]{1,0:T(8,128)S(1)} %get-tuple-element.35), channel_id=1, source_target_pairs={{2,4},{6,8},{10,12},{4,2},{8,6},{12,10},{3,5},{7,9},{11,13},{5,3},... | collective-permute-start | bytes 786440 | tf_op jit(solution)/shard_map/ppermute | solution.py:545
  7.7 7.8 %advance_step.1 = (f32[8192,128]{1,0:T(8,128)S(1)}, f32[8192,128]{1,0:T(8,128)}, f32[512,128]{1,0:T(8,128)S(1)}, f32[512,128]{1,0:T(8,128)S(1)}, f32[512,128]{1,...) custom-call(s32[4,128]{1,0:T(4,128)S(1)} %get-tuple-element.26.words, ...), custom_call_target="tpu_custom_call", output_to_operand_aliasing={{7}: (3, {})} | custom-call | bytes 20971520 | tf_op jit(solution)/shard_map/advance_step/pallas_call | solution.py:547
  15.5 0.2 %collective-permute-start.2 = (f32[512,128]{1,0:T(8,128)S(1)}, f32[512,128]{1,0:T(8,128)S(1)}, u32[]{:S(2)}, u32[]{:S(2)}) collective-permute-start(f32[512,128]{1,0:T(8,128)S(1)} %get-tuple-element.41), channel_id=1, source_target_pairs={{0,16},{16,0},{1,17},{17,1},{2,18},{18,2},{3,19},{19,3},{4,20},{20... | collective-permute-start | bytes 786440 | tf_op jit(solution)/shard_map/ppermute | solution.py:567
  15.7 0.0 collective-permute-done.1.refs_0_
  15.8 0.0 collective-permute-done.refs_1_
  15.8 0.9 %ghost_send.1 = (f32[3080,128]{1,0:T(8,128)S(1)}, f32[512,128]{1,0:T(8,128)S(1)}, f32[8192,128]{1,0:T(8,128)S(1)}, f32[512,128]{1,0:T(8,128)S(1)}) custom-call(s32[520]{0:T(1024)S(4)} %get-tuple-element.33.refs_0_.ghosts, f32[512,128]{1,0:T(8,128)S(1)} %collective-permute-done.refs_1_, ...), custom_call_target="tpu_custom_call", output_to_operand_aliasing={{0}: (5, {}), {1}: (6, {}), {2}: (7, {}), {3}: (8, {})} | custom-call | bytes 1048576 | tf_op jit(solution)/shard_map/ghost_send/pallas_call | solution.py:580
  16.7 1.5 %collective-permute-start.3 = (f32[512,128]{1,0:T(8,128)S(1)}, f32[512,128]{1,0:T(8,128)S(1)}, u32[]{:S(2)}, u32[]{:S(2)}) collective-permute-start(f32[512,128]{1,0:T(8,128)S(1)} %get-tuple-element.47), channel_id=1, source_target_pairs={{0,16},{16,0},{1,17},{17,1},{2,18},{18,2},{3,19},{19,3},{4,20},{20... | collective-permute-start | bytes 786440 | tf_op jit(solution)/shard_map/ppermute | solution.py:596
  18.2 0.0 collective-permute-done.2.partner_mid
  18.2 1.1 %ghost_fix.1 = (f32[8192,128]{1,0:T(8,128)S(1)}, f32[512,128]{1,0:T(8,128)S(1)}, f32[8192,128]{1,0:T(8,128)}, f32[1024,128]{1,0:T(8,128)S(1)}) custom-call(s32[520]{0:T(1024)S(4)} %get-tuple-element.33.refs_0_.ghosts, f32[2048,128]{1,0:T(8,128)S(1)} %get-tuple-element.34.refs_2_.rates, ...), custom_call_target="tpu_custom_call", output_to_operand_aliasing={{0}: (6, {}), {1}: (7, {}), {2}: (8, {})} | custom-call | bytes 4194304 | tf_op jit(solution)/shard_map/ghost_fix/pallas_call | solution.py:598
  19.3 0.0 collective-permute-done.3.partner
  19.3 0.8 %level_gap.1 = (f32[1024,128]{1,0:T(8,128)S(1)}, f32[1024,128]{1,0:T(8,128)}) custom-call(f32[512,128]{1,0:T(8,128)S(1)} %get-tuple-element.46.kept, f32[512,128]{1,0:T(8,128)S(1)} %collective-permute-done.3.partner, f32[1024,128]{1,0:T(8,128)S(1)} %get-tuple-element.48.rows_in), custom_call_target="tpu_custom_call", output_to_operand_aliasing={{0}: (2, {})} | custom-call | bytes 1048576 | tf_op jit(solution)/shard_map/level_gap/pallas_call | solution.py:618
  (1 shorter events, 0.0 us)
Async XLA Ops:
  3.2 12.5 %collective-permute-start.1 = (f32[512,128]{1,0:T(8,128)S(1)}, f32[512,128]{1,0:T(8,128)S(1)}, u32[]{:S(2)}, u32[]{:S(2)}) collective-permute-start(f32[512,128]{1,0:T(8,128)S(1)} %get-tuple-element.35), channel_id=1, source_target_pairs={{0,2},{2,0},{4,6},{6,4},{8,10},{10,8},{12,14},{14,12},{1,3},{3,1},... | collective-permute-start | bytes 786440 | tf_op jit(solution)/shard_map/ppermute | solution.py:544
  3.5 12.2 %collective-permute-start = (f32[512,128]{1,0:T(8,128)S(1)}, f32[512,128]{1,0:T(8,128)S(1)}, u32[]{:S(2)}, u32[]{:S(2)}) collective-permute-start(f32[512,128]{1,0:T(8,128)S(1)} %get-tuple-element.35), channel_id=1, source_target_pairs={{2,4},{6,8},{10,12},{4,2},{8,6},{12,10},{3,5},{7,9},{11,13},{5,3},... | collective-permute-start | bytes 786440 | tf_op jit(solution)/shard_map/ppermute | solution.py:545
  15.5 2.7 %collective-permute-start.2 = (f32[512,128]{1,0:T(8,128)S(1)}, f32[512,128]{1,0:T(8,128)S(1)}, u32[]{:S(2)}, u32[]{:S(2)}) collective-permute-start(f32[512,128]{1,0:T(8,128)S(1)} %get-tuple-element.41), channel_id=1, source_target_pairs={{0,16},{16,0},{1,17},{17,1},{2,18},{18,2},{3,19},{19,3},{4,20},{20... | collective-permute-start | bytes 786440 | tf_op jit(solution)/shard_map/ppermute | solution.py:567
  16.7 2.7 %collective-permute-start.3 = (f32[512,128]{1,0:T(8,128)S(1)}, f32[512,128]{1,0:T(8,128)S(1)}, u32[]{:S(2)}, u32[]{:S(2)}) collective-permute-start(f32[512,128]{1,0:T(8,128)S(1)} %get-tuple-element.47), channel_id=1, source_target_pairs={{0,16},{16,0},{1,17},{17,1},{2,18},{18,2},{3,19},{19,3},{4,20},{20... | collective-permute-start | bytes 786440 | tf_op jit(solution)/shard_map/ppermute | solution.py:596

commit v7 on v6

--- a/solution.py
+++ b/solution.py
@@ -177,11 +177,17 @@
             dest[pl.ds(start + 4 * u, 4), :] = tiles[u]
 
 
-def list_eight(q, words, ghosts, count):
+def list_eight(fine, q, words, ghosts, counts):
+    count, turned = counts
+    second = ghosts.shape[0] // 2
     for w in eight_words(q, words):
+        fed = lax.shift_right_logical(w, 31)
         ghosts[count] = w
-        count = count + lax.shift_right_logical(w, 31)
-    return count
+        count = count + fed
+        if fine:
+            ghosts[second + turned] = w
+            turned = turned + (fed & (w >> 20))
+    return count, turned
 
 
 def fine_block(q, cells, rates, factor, boosts, flow_back, ahead_in, new, shares):
@@ -273,7 +279,7 @@
                 )
             later = jnp.minimum(q + 1, eights - 1)
             gather_eight(fine, later, words, outflow, ahead_in, behind_in)
-            return list_eight(q, words, ghosts, count)
+            return list_eight(fine, q, words, ghosts, count)
 
         per = eights // parts
 
@@ -287,7 +293,9 @@
 
             return count
 
-        ghosts[8 * eights] = lax.fori_loop(0, parts, part, jnp.int32(0))
+        count, turned = lax.fori_loop(0, parts, part, (jnp.int32(0), jnp.int32(0)))
+        ghosts[8 * eights] = count
+        ghosts[16 * eights + 8] = turned
 
     @pl.when(level == 0)
     def _():
@@ -309,16 +317,16 @@
     outflow[pl.ds(start, half), :] = arrived[...]
 
 
-def over_list(count, ghosts, width, each):
+def over_list(count, ghosts, width, each, first=0):
     whole = count // width
 
     @pl.loop(0, whole)
     def _(m):
-        each([ghosts[m * width + u] for u in range(width)])
+        each([ghosts[first + m * width + u] for u in range(width)])
 
     @pl.loop(whole * width, count)
     def _(i):
-        each([ghosts[i]])
+        each([ghosts[first + i]])
 
 
 def send_kernel(
@@ -332,15 +340,14 @@
     def fine(entries):
         done = []
         for w in entries:
-            src, p, rev = w & 1023, w >> 10 & 1023, w >> 20 & 1
+            src, p = w & 1023, w >> 10 & 1023
             own = pl.ds(p, 1)
             rows = outflow[pl.ds(pl.multiple_of(src * 4, 4), 4), :]
             f, r = factor[own, :], rates[pl.ds(p * 4, 1), :]
             total = rows[0:1]
             for s in range(1, GROUPS):
                 total = f * total + rows[s : s + 1]
-            back = jnp.where(rev == 1, jnp.float32(0.25), jnp.float32(0.0))
-            done.append((own, sent[own, :] + f * r * total * back))
+            done.append((own, sent[own, :] + f * r * total * 0.25))
         for own, row in done:
             sent[own, :] = row
 
@@ -349,7 +356,7 @@
 
     @pl.when(level == 0)
     def _():
-        over_list(ghosts[pipes], ghosts, 8, fine)
+        over_list(ghosts[2 * pipes + 8], ghosts, 4, fine, pipes + 8)
 
     @pl.when(level == 1)
     def _():
@@ -553,7 +560,7 @@
             pltpu.VMEM((pipes * SEGF, columns), f32),
             jax.ShapeDtypeStruct((pipes * SEGF, columns), f32),
             *[pltpu.VMEM((pipes, columns), f32)] * 4,
-            pltpu.SMEM((pipes + 8,), i32),
+            pltpu.SMEM((2 * (pipes + 8),), i32),
             pltpu.VMEM((pipes * GROUPS, columns), f32),
         ],
         scratch_shapes=[pltpu.VMEM((GROUPS * pipes, columns), f32)] * 2

time: 20.4 us -> 20.3 us (level)
  the two profiles are of different devices: /device:TPU:11 before, /device:TPU:0 now
where the time goes in v7:
time: 20.3 us; the launch traced here: 20 us
  Pallas kernels  12.4 us (61%)
  starting transfers between devices  3.84 us (19%)
  waiting for transfers between devices  3.1 us (15%)
  between operations  0.71 us (3%)
    pallas_call x1, Pallas kernels, per_device(): pl.pallas_call(step_kernel, name='advance_step', in_specs=[SMEM, HBM] + [...  6.98 us
    ppermute x1, waiting for transfers between devices, per_device(): near_rows = lax.ppermute(face_rows, 'dom', near_pairs)  3.09 us
    ppermute x1, starting transfers between devices, per_device(): near_rows = lax.ppermute(face_rows, 'dom', near_pairs)  3 us
    pallas_call x1, Pallas kernels, per_device(): pl.pallas_call(load_kernel, name='load_step', in_specs=[HBM] * 7, out_spe...  2.9 us
    pallas_call x1, Pallas kernels, per_device(): pl.pallas_call(fix_kernel, name='ghost_fix', in_specs=[SMEM] + [VMEM] * 7...  1.5 us
    pallas_call x1, Pallas kernels, per_device(): pl.pallas_call(gap_kernel, name='level_gap', in_specs=[VMEM] * 3, out_spe...  0.83 us
    ppermute x1, starting transfers between devices, per_device(): far_rows = lax.ppermute(face_rows, 'dom', far_pairs)  0.67 us
  transfers between devices with their start and end apart: 4, of which 1 were waited for; matrix products, arithmetic and copies ran while one was open for 0% of the time, Pallas kernels for 43%

profile of v7, /device:TPU:0, one launch (start us, length us, event | category | flops | bytes accessed | tf_op | source)
XLA Modules:
  0.0 20.0 jit_solution(12386536569321099109)
XLA Ops:
  0.6 2.9 %load_step.1 = (f32[8192,128]{1,0:T(8,128)S(1)}, f32[2048,128]{1,0:T(8,128)S(1)}, f32[3080,128]{1,0:T(8,128)S(1)}, f32[512,128]{1,0:T(8,128)S(1)}, f32[512,128]{...) custom-call(f32[8192,128]{1,0:T(8,128)} %bitcast.15, ...), custom_call_target="tpu_custom_call" | custom-call | bytes 5242880 | tf_op jit(solution)/shard_map/load_step/pallas_call | solution.py:519
  3.5 3.0 %collective-permute-start.1 = (f32[512,128]{1,0:T(8,128)S(1)}, f32[512,128]{1,0:T(8,128)S(1)}, u32[]{:S(2)}, u32[]{:S(2)}) collective-permute-start(f32[512,128]{1,0:T(8,128)S(1)} %get-tuple-element.35), channel_id=1, source_target_pairs={{0,2},{2,0},{4,6},{6,4},{8,10},{10,8},{12,14},{14,12},{1,3},{3,1},... | collective-permute-start | bytes 786440 | tf_op jit(solution)/shard_map/ppermute | solution.py:551
  6.5 0.7 %collective-permute-start = (f32[512,128]{1,0:T(8,128)S(1)}, f32[512,128]{1,0:T(8,128)S(1)}, u32[]{:S(2)}, u32[]{:S(2)}) collective-permute-start(f32[512,128]{1,0:T(8,128)S(1)} %get-tuple-element.35), channel_id=1, source_target_pairs={{2,4},{6,8},{10,12},{4,2},{8,6},{12,10},{3,5},{7,9},{11,13},{5,3},... | collective-permute-start | bytes 786440 | tf_op jit(solution)/shard_map/ppermute | solution.py:552
  7.2 7.0 %advance_step.1 = (f32[8192,128]{1,0:T(8,128)S(1)}, f32[8192,128]{1,0:T(8,128)}, f32[512,128]{1,0:T(8,128)S(1)}, f32[512,128]{1,0:T(8,128)S(1)}, f32[512,128]{1,...) custom-call(s32[4,128]{1,0:T(4,128)S(1)} %get-tuple-element.26.words, ...), custom_call_target="tpu_custom_call", output_to_operand_aliasing={{7}: (3, {})} | custom-call | bytes 20971520 | tf_op jit(solution)/shard_map/advance_step/pallas_call | solution.py:554
  14.2 0.1 collective-permute-start.2
  14.3 3.1 %collective-permute-done.1.refs_0_ = f32[512,128]{1,0:T(8,128)S(1)} collective-permute-done((f32[512,128]{1,0:T(8,128)S(1)}, f32[512,128]{1,0:T(8,128)S(1)}, u32[]{:S(2)}, u32[]{:S(2)}) %collective-permute-start.1) | collective-permute-done | bytes 262176 | tf_op jit(solution)/shard_map/ppermute | solution.py:551
  17.4 0.0 collective-permute-done.refs_1_
  17.4 0.1 ghost_send.1
  17.6 0.1 collective-permute-start.3
  17.7 0.0 collective-permute-done.2.partner_mid
  17.7 1.5 %ghost_fix.1 = (f32[8192,128]{1,0:T(8,128)S(1)}, f32[512,128]{1,0:T(8,128)S(1)}, f32[8192,128]{1,0:T(8,128)}, f32[1024,128]{1,0:T(8,128)S(1)}) custom-call(s32[1040]{0:T(1024)S(4)} %get-tuple-element.33.refs_0_.ghosts, f32[2048,128]{1,0:T(8,128)S(1)} %get-tuple-element.34.refs_2_.rates, ...), custom_call_target="tpu_custom_call", output_to_operand_aliasing={{0}: (6, {}), {1}: (7, {}), {2}: (8, {})} | custom-call | bytes 4194304 | tf_op jit(solution)/shard_map/ghost_fix/pallas_call | solution.py:605
  19.2 0.0 collective-permute-done.3.partner
  19.2 0.8 %level_gap.1 = (f32[1024,128]{1,0:T(8,128)S(1)}, f32[1024,128]{1,0:T(8,128)}) custom-call(f32[512,128]{1,0:T(8,128)S(1)} %get-tuple-element.46.kept, f32[512,128]{1,0:T(8,128)S(1)} %collective-permute-done.3.partner, f32[1024,128]{1,0:T(8,128)S(1)} %get-tuple-element.48.rows_in), custom_call_target="tpu_custom_call", output_to_operand_aliasing={{0}: (2, {})} | custom-call | bytes 1048576 | tf_op jit(solution)/shard_map/level_gap/pallas_call | solution.py:625
  (1 shorter events, 0.0 us)
Async XLA Ops:
  3.5 13.9 %collective-permute-start.1 = (f32[512,128]{1,0:T(8,128)S(1)}, f32[512,128]{1,0:T(8,128)S(1)}, u32[]{:S(2)}, u32[]{:S(2)}) collective-permute-start(f32[512,128]{1,0:T(8,128)S(1)} %get-tuple-element.35), channel_id=1, source_target_pairs={{0,2},{2,0},{4,6},{6,4},{8,10},{10,8},{12,14},{14,12},{1,3},{3,1},... | collective-permute-start | bytes 786440 | tf_op jit(solution)/shard_map/ppermute | solution.py:551
  6.5 10.9 %collective-permute-start = (f32[512,128]{1,0:T(8,128)S(1)}, f32[512,128]{1,0:T(8,128)S(1)}, u32[]{:S(2)}, u32[]{:S(2)}) collective-permute-start(f32[512,128]{1,0:T(8,128)S(1)} %get-tuple-element.35), channel_id=1, source_target_pairs={{2,4},{6,8},{10,12},{4,2},{8,6},{12,10},{3,5},{7,9},{11,13},{5,3},... | collective-permute-start | bytes 786440 | tf_op jit(solution)/shard_map/ppermute | solution.py:552
  14.2 3.5 %collective-permute-start.2 = (f32[512,128]{1,0:T(8,128)S(1)}, f32[512,128]{1,0:T(8,128)S(1)}, u32[]{:S(2)}, u32[]{:S(2)}) collective-permute-start(f32[512,128]{1,0:T(8,128)S(1)} %get-tuple-element.41), channel_id=1, source_target_pairs={{0,16},{16,0},{1,17},{17,1},{2,18},{18,2},{3,19},{19,3},{4,20},{20... | collective-permute-start | bytes 786440 | tf_op jit(solution)/shard_map/ppermute | solution.py:574
  17.6 1.6 %collective-permute-start.3 = (f32[512,128]{1,0:T(8,128)S(1)}, f32[512,128]{1,0:T(8,128)S(1)}, u32[]{:S(2)}, u32[]{:S(2)}) collective-permute-start(f32[512,128]{1,0:T(8,128)S(1)} %get-tuple-element.47), channel_id=1, source_target_pairs={{0,16},{16,0},{1,17},{17,1},{2,18},{18,2},{3,19},{19,3},{4,20},{20... | collective-permute-start | bytes 786440 | tf_op jit(solution)/shard_map/ppermute | solution.py:603

commit v8 on v7

--- a/solution.py
+++ b/solution.py
@@ -150,13 +150,13 @@
                         cells[pl.ds(base + 4 * g + 3, 8, stride=16), :],
                     )
 
-    @pl.loop(0, faces.shape[0] // 16)
+    @pl.loop(0, faces.shape[0] // 64)
     def _(m):
         moved = [
-            outflow[pl.ds(pl.multiple_of(face_s[m * 16 + u] * 4, 4), 4), :] for u in range(16)
+            outflow[pl.ds(pl.multiple_of(face_s[m * 64 + u] * 4, 4), 4), :] for u in range(64)
         ]
-        for u in range(16):
-            face_rows[pl.ds(pl.multiple_of(m * 64, 64) + 4 * u, 4), :] = moved[u]
+        for u in range(64):
+            face_rows[pl.ds(pl.multiple_of(m * 256, 256) + 4 * u, 4), :] = moved[u]
 
 
 def eight_words(q, words):

time: 20.3 us -> 20.2 us (level)
  the two profiles are of different devices: /device:TPU:0 before, /device:TPU:11 now
where the time goes in v8:
time: 20.2 us; the launch traced here: 19.8 us
  Pallas kernels  13 us (64%)
  starting transfers between devices  6.08 us (30%)
  between operations  0.69 us (3%)
    pallas_call x1, Pallas kernels, per_device(): pl.pallas_call(step_kernel, name='advance_step', in_specs=[SMEM, HBM] + [...  7.79 us
    ppermute x1, starting transfers between devices, per_device(): far_rows = lax.ppermute(face_rows, 'dom', far_pairs)  4.12 us
    pallas_call x1, Pallas kernels, per_device(): pl.pallas_call(load_kernel, name='load_step', in_specs=[HBM] * 7, out_spe...  2.55 us
    pallas_call x1, Pallas kernels, per_device(): pl.pallas_call(fix_kernel, name='ghost_fix', in_specs=[SMEM] + [VMEM] * 7...  1.08 us
    pallas_call x1, Pallas kernels, per_device(): pl.pallas_call(gap_kernel, name='level_gap', in_specs=[VMEM] * 3, out_spe...  0.83 us
    ppermute x1, starting transfers between devices, per_device(): partner = lax.ppermute(sent, 'level', swap)  0.82 us
    ppermute x1, starting transfers between devices, per_device(): partner_mid = lax.ppermute(sent_mid, 'level', swap)  0.82 us
    pallas_call x1, Pallas kernels, per_device(): pl.pallas_call(lambda *refs: send_kernel(first, *refs), name='ghost_send'...  0.72 us
  transfers between devices with their start and end apart: 4, of which 1 were waited for; matrix products, arithmetic and copies ran while one was open for 0% of the time, Pallas kernels for 49%

profile of v8, /device:TPU:11, one launch (start us, length us, event | category | flops | bytes accessed | tf_op | source)
XLA Modules:
  0.0 19.8 jit_solution(10298575321084974281)
XLA Ops:
  0.6 2.5 %load_step.1 = (f32[8192,128]{1,0:T(8,128)S(1)}, f32[2048,128]{1,0:T(8,128)S(1)}, f32[3080,128]{1,0:T(8,128)S(1)}, f32[512,128]{1,0:T(8,128)S(1)}, f32[512,128]{...) custom-call(f32[8192,128]{1,0:T(8,128)} %bitcast.15, ...), custom_call_target="tpu_custom_call" | custom-call | bytes 5242880 | tf_op jit(solution)/shard_map/load_step/pallas_call | solution.py:519
  3.2 0.3 %collective-permute-start.1 = (f32[512,128]{1,0:T(8,128)S(1)}, f32[512,128]{1,0:T(8,128)S(1)}, u32[]{:S(2)}, u32[]{:S(2)}) collective-permute-start(f32[512,128]{1,0:T(8,128)S(1)} %get-tuple-element.35), channel_id=1, source_target_pairs={{0,2},{2,0},{4,6},{6,4},{8,10},{10,8},{12,14},{14,12},{1,3},{3,1},... | collective-permute-start | bytes 786440 | tf_op jit(solution)/shard_map/ppermute | solution.py:551
  3.5 4.1 %collective-permute-start = (f32[512,128]{1,0:T(8,128)S(1)}, f32[512,128]{1,0:T(8,128)S(1)}, u32[]{:S(2)}, u32[]{:S(2)}) collective-permute-start(f32[512,128]{1,0:T(8,128)S(1)} %get-tuple-element.35), channel_id=1, source_target_pairs={{2,4},{6,8},{10,12},{4,2},{8,6},{12,10},{3,5},{7,9},{11,13},{5,3},... | collective-permute-start | bytes 786440 | tf_op jit(solution)/shard_map/ppermute | solution.py:552
  7.6 7.8 %advance_step.1 = (f32[8192,128]{1,0:T(8,128)S(1)}, f32[8192,128]{1,0:T(8,128)}, f32[512,128]{1,0:T(8,128)S(1)}, f32[512,128]{1,0:T(8,128)S(1)}, f32[512,128]{1,...) custom-call(s32[4,128]{1,0:T(4,128)S(1)} %get-tuple-element.26.words, ...), custom_call_target="tpu_custom_call", output_to_operand_aliasing={{7}: (3, {})} | custom-call | bytes 20971520 | tf_op jit(solution)/shard_map/advance_step/pallas_call | solution.py:554
  15.4 0.8 %collective-permute-start.2 = (f32[512,128]{1,0:T(8,128)S(1)}, f32[512,128]{1,0:T(8,128)S(1)}, u32[]{:S(2)}, u32[]{:S(2)}) collective-permute-start(f32[512,128]{1,0:T(8,128)S(1)} %get-tuple-element.41), channel_id=1, source_target_pairs={{0,16},{16,0},{1,17},{17,1},{2,18},{18,2},{3,19},{19,3},{4,20},{20... | collective-permute-start | bytes 786440 | tf_op jit(solution)/shard_map/ppermute | solution.py:574
  16.3 0.0 collective-permute-done.1.refs_0_
  16.3 0.0 collective-permute-done.refs_1_
  16.3 0.7 %ghost_send.1 = (f32[3080,128]{1,0:T(8,128)S(1)}, f32[512,128]{1,0:T(8,128)S(1)}, f32[8192,128]{1,0:T(8,128)S(1)}, f32[512,128]{1,0:T(8,128)S(1)}) custom-call(s32[1040]{0:T(1024)S(4)} %get-tuple-element.33.refs_0_.ghosts, f32[512,128]{1,0:T(8,128)S(1)} %collective-permute-done.refs_1_, ...), custom_call_target="tpu_custom_call", output_to_operand_aliasing={{0}: (5, {}), {1}: (6, {}), {2}: (7, {}), {3}: (8, {})} | custom-call | bytes 1048576 | tf_op jit(solution)/shard_map/ghost_send/pallas_call | solution.py:587
  17.0 0.8 %collective-permute-start.3 = (f32[512,128]{1,0:T(8,128)S(1)}, f32[512,128]{1,0:T(8,128)S(1)}, u32[]{:S(2)}, u32[]{:S(2)}) collective-permute-start(f32[512,128]{1,0:T(8,128)S(1)} %get-tuple-element.47), channel_id=1, source_target_pairs={{0,16},{16,0},{1,17},{17,1},{2,18},{18,2},{3,19},{19,3},{4,20},{20... | collective-permute-start | bytes 786440 | tf_op jit(solution)/shard_map/ppermute | solution.py:603
  17.9 0.0 collective-permute-done.2.partner_mid
  17.9 1.1 %ghost_fix.1 = (f32[8192,128]{1,0:T(8,128)S(1)}, f32[512,128]{1,0:T(8,128)S(1)}, f32[8192,128]{1,0:T(8,128)}, f32[1024,128]{1,0:T(8,128)S(1)}) custom-call(s32[1040]{0:T(1024)S(4)} %get-tuple-element.33.refs_0_.ghosts, f32[2048,128]{1,0:T(8,128)S(1)} %get-tuple-element.34.refs_2_.rates, ...), custom_call_target="tpu_custom_call", output_to_operand_aliasing={{0}: (6, {}), {1}: (7, {}), {2}: (8, {})} | custom-call | bytes 4194304 | tf_op jit(solution)/shard_map/ghost_fix/pallas_call | solution.py:605
  18.9 0.1 collective-permute-done.3.partner
  19.0 0.8 %level_gap.1 = (f32[1024,128]{1,0:T(8,128)S(1)}, f32[1024,128]{1,0:T(8,128)}) custom-call(f32[512,128]{1,0:T(8,128)S(1)} %get-tuple-element.46.kept, f32[512,128]{1,0:T(8,128)S(1)} %collective-permute-done.3.partner, f32[1024,128]{1,0:T(8,128)S(1)} %get-tuple-element.48.rows_in), custom_call_target="tpu_custom_call", output_to_operand_aliasing={{0}: (2, {})} | custom-call | bytes 1048576 | tf_op jit(solution)/shard_map/level_gap/pallas_call | solution.py:625
  (1 shorter events, 0.0 us)
Async XLA Ops:
  3.2 13.1 %collective-permute-start.1 = (f32[512,128]{1,0:T(8,128)S(1)}, f32[512,128]{1,0:T(8,128)S(1)}, u32[]{:S(2)}, u32[]{:S(2)}) collective-permute-start(f32[512,128]{1,0:T(8,128)S(1)} %get-tuple-element.35), channel_id=1, source_target_pairs={{0,2},{2,0},{4,6},{6,4},{8,10},{10,8},{12,14},{14,12},{1,3},{3,1},... | collective-permute-start | bytes 786440 | tf_op jit(solution)/shard_map/ppermute | solution.py:551
  3.5 12.8 %collective-permute-start = (f32[512,128]{1,0:T(8,128)S(1)}, f32[512,128]{1,0:T(8,128)S(1)}, u32[]{:S(2)}, u32[]{:S(2)}) collective-permute-start(f32[512,128]{1,0:T(8,128)S(1)} %get-tuple-element.35), channel_id=1, source_target_pairs={{2,4},{6,8},{10,12},{4,2},{8,6},{12,10},{3,5},{7,9},{11,13},{5,3},... | collective-permute-start | bytes 786440 | tf_op jit(solution)/shard_map/ppermute | solution.py:552
  15.4 2.4 %collective-permute-start.2 = (f32[512,128]{1,0:T(8,128)S(1)}, f32[512,128]{1,0:T(8,128)S(1)}, u32[]{:S(2)}, u32[]{:S(2)}) collective-permute-start(f32[512,128]{1,0:T(8,128)S(1)} %get-tuple-element.41), channel_id=1, source_target_pairs={{0,16},{16,0},{1,17},{17,1},{2,18},{18,2},{3,19},{19,3},{4,20},{20... | collective-permute-start | bytes 786440 | tf_op jit(solution)/shard_map/ppermute | solution.py:574
  17.0 2.0 %collective-permute-start.3 = (f32[512,128]{1,0:T(8,128)S(1)}, f32[512,128]{1,0:T(8,128)S(1)}, u32[]{:S(2)}, u32[]{:S(2)}) collective-permute-start(f32[512,128]{1,0:T(8,128)S(1)} %get-tuple-element.47), channel_id=1, source_target_pairs={{0,16},{16,0},{1,17},{17,1},{2,18},{18,2},{3,19},{19,3},{4,20},{20... | collective-permute-start | bytes 786440 | tf_op jit(solution)/shard_map/ppermute | solution.py:603

commit v9 on v7

--- a/solution.py
+++ b/solution.py
@@ -489,9 +489,14 @@
     copies = []
     per = kept.shape[0] // 8 // parts
     for n in range(parts):
-        for q in range(n * per, (n + 1) * per):
-            own = pl.ds(8 * q, 8)
-            rows[pl.ds(16 * q + level, 8, stride=2), :] = (kept[own, :] - partner[own, :]) * sign
+        @pl.loop(0, per // 8)
+        def _(m):
+            for u in range(8):
+                at = pl.multiple_of(n * per * 8 + m * 64 + 8 * u, 8)
+                own = pl.ds(at, 8)
+                spots = pl.ds(pl.multiple_of(2 * at, 16) + level, 8, stride=2)
+                rows[spots, :] = (kept[own, :] - partner[own, :]) * sign
+
         part = pl.ds(n * per * 16, per * 16)
         copies.append(pltpu.make_async_copy(rows.at[part], gap.at[part], sems.at[n]))
         copies[-1].start()

time: 20.3 us -> 20.3 us (level)
  the two profiles are of different devices: /device:TPU:0 before, /device:TPU:11 now
where the time goes in v9:
time: 20.3 us; the launch traced here: 19.9 us
  Pallas kernels  13.2 us (65%)
  starting transfers between devices  5.99 us (30%)
  between operations  0.69 us (3%)
    pallas_call x1, Pallas kernels, per_device(): pl.pallas_call(step_kernel, name='advance_step', in_specs=[SMEM, HBM] + [...  7.79 us
    ppermute x1, starting transfers between devices, per_device(): far_rows = lax.ppermute(face_rows, 'dom', far_pairs)  4.12 us
    pallas_call x1, Pallas kernels, per_device(): pl.pallas_call(load_kernel, name='load_step', in_specs=[HBM] * 7, out_spe...  2.58 us
    pallas_call x1, Pallas kernels, per_device(): pl.pallas_call(fix_kernel, name='ghost_fix', in_specs=[SMEM] + [VMEM] * 7...  1.14 us
    pallas_call x1, Pallas kernels, per_device(): pl.pallas_call(lambda *refs: send_kernel(first, *refs), name='ghost_send'...  0.84 us
    pallas_call x1, Pallas kernels, per_device(): pl.pallas_call(gap_kernel, name='level_gap', in_specs=[VMEM] * 3, out_spe...  0.84 us
    ppermute x1, starting transfers between devices, per_device(): partner_mid = lax.ppermute(sent_mid, 'level', swap)  0.82 us
    ppermute x1, starting transfers between devices, per_device(): partner = lax.ppermute(sent, 'level', swap)  0.73 us
  transfers between devices with their start and end apart: 4, of which 0 were waited for; matrix products, arithmetic and copies ran while one was open for 0% of the time, Pallas kernels for 49%

profile of v9, /device:TPU:11, one launch (start us, length us, event | category | flops | bytes accessed | tf_op | source)
XLA Modules:
  0.0 19.9 jit_solution(13503517394877332300)
XLA Ops:
  0.6 2.6 %load_step.1 = (f32[8192,128]{1,0:T(8,128)S(1)}, f32[2048,128]{1,0:T(8,128)S(1)}, f32[3080,128]{1,0:T(8,128)S(1)}, f32[512,128]{1,0:T(8,128)S(1)}, f32[512,128]{...) custom-call(f32[8192,128]{1,0:T(8,128)} %bitcast.15, ...), custom_call_target="tpu_custom_call" | custom-call | bytes 5242880 | tf_op jit(solution)/shard_map/load_step/pallas_call | solution.py:524
  3.2 0.3 %collective-permute-start.1 = (f32[512,128]{1,0:T(8,128)S(1)}, f32[512,128]{1,0:T(8,128)S(1)}, u32[]{:S(2)}, u32[]{:S(2)}) collective-permute-start(f32[512,128]{1,0:T(8,128)S(1)} %get-tuple-element.35), channel_id=1, source_target_pairs={{0,2},{2,0},{4,6},{6,4},{8,10},{10,8},{12,14},{14,12},{1,3},{3,1},... | collective-permute-start | bytes 786440 | tf_op jit(solution)/shard_map/ppermute | solution.py:556
  3.5 4.1 %collective-permute-start = (f32[512,128]{1,0:T(8,128)S(1)}, f32[512,128]{1,0:T(8,128)S(1)}, u32[]{:S(2)}, u32[]{:S(2)}) collective-permute-start(f32[512,128]{1,0:T(8,128)S(1)} %get-tuple-element.35), channel_id=1, source_target_pairs={{2,4},{6,8},{10,12},{4,2},{8,6},{12,10},{3,5},{7,9},{11,13},{5,3},... | collective-permute-start | bytes 786440 | tf_op jit(solution)/shard_map/ppermute | solution.py:557
  7.7 7.8 %advance_step.1 = (f32[8192,128]{1,0:T(8,128)S(1)}, f32[8192,128]{1,0:T(8,128)}, f32[512,128]{1,0:T(8,128)S(1)}, f32[512,128]{1,0:T(8,128)S(1)}, f32[512,128]{1,...) custom-call(s32[4,128]{1,0:T(4,128)S(1)} %get-tuple-element.26.words, ...), custom_call_target="tpu_custom_call", output_to_operand_aliasing={{7}: (3, {})} | custom-call | bytes 20971520 | tf_op jit(solution)/shard_map/advance_step/pallas_call | solution.py:559
  15.5 0.8 %collective-permute-start.2 = (f32[512,128]{1,0:T(8,128)S(1)}, f32[512,128]{1,0:T(8,128)S(1)}, u32[]{:S(2)}, u32[]{:S(2)}) collective-permute-start(f32[512,128]{1,0:T(8,128)S(1)} %get-tuple-element.41), channel_id=1, source_target_pairs={{0,16},{16,0},{1,17},{17,1},{2,18},{18,2},{3,19},{19,3},{4,20},{20... | collective-permute-start | bytes 786440 | tf_op jit(solution)/shard_map/ppermute | solution.py:579
  16.3 0.0 collective-permute-done.1.refs_0_
  16.3 0.0 collective-permute-done.refs_1_
  16.3 0.8 %ghost_send.1 = (f32[3080,128]{1,0:T(8,128)S(1)}, f32[512,128]{1,0:T(8,128)S(1)}, f32[8192,128]{1,0:T(8,128)S(1)}, f32[512,128]{1,0:T(8,128)S(1)}) custom-call(s32[1040]{0:T(1024)S(4)} %get-tuple-element.33.refs_0_.ghosts, f32[512,128]{1,0:T(8,128)S(1)} %collective-permute-done.refs_1_, ...), custom_call_target="tpu_custom_call", output_to_operand_aliasing={{0}: (5, {}), {1}: (6, {}), {2}: (7, {}), {3}: (8, {})} | custom-call | bytes 1048576 | tf_op jit(solution)/shard_map/ghost_send/pallas_call | solution.py:592
  17.2 0.7 %collective-permute-start.3 = (f32[512,128]{1,0:T(8,128)S(1)}, f32[512,128]{1,0:T(8,128)S(1)}, u32[]{:S(2)}, u32[]{:S(2)}) collective-permute-start(f32[512,128]{1,0:T(8,128)S(1)} %get-tuple-element.47), channel_id=1, source_target_pairs={{0,16},{16,0},{1,17},{17,1},{2,18},{18,2},{3,19},{19,3},{4,20},{20... | collective-permute-start | bytes 786440 | tf_op jit(solution)/shard_map/ppermute | solution.py:608
  17.9 0.0 collective-permute-done.2.partner_mid
  17.9 1.1 %ghost_fix.1 = (f32[8192,128]{1,0:T(8,128)S(1)}, f32[512,128]{1,0:T(8,128)S(1)}, f32[8192,128]{1,0:T(8,128)}, f32[1024,128]{1,0:T(8,128)S(1)}) custom-call(s32[1040]{0:T(1024)S(4)} %get-tuple-element.33.refs_0_.ghosts, f32[2048,128]{1,0:T(8,128)S(1)} %get-tuple-element.34.refs_2_.rates, ...), custom_call_target="tpu_custom_call", output_to_operand_aliasing={{0}: (6, {}), {1}: (7, {}), {2}: (8, {})} | custom-call | bytes 4194304 | tf_op jit(solution)/shard_map/ghost_fix/pallas_call | solution.py:610
  19.1 0.0 collective-permute-done.3.partner
  19.1 0.8 %level_gap.1 = (f32[1024,128]{1,0:T(8,128)S(1)}, f32[1024,128]{1,0:T(8,128)}) custom-call(f32[512,128]{1,0:T(8,128)S(1)} %get-tuple-element.46.kept, f32[512,128]{1,0:T(8,128)S(1)} %collective-permute-done.3.partner, f32[1024,128]{1,0:T(8,128)S(1)} %get-tuple-element.48.rows_in), custom_call_target="tpu_custom_call", output_to_operand_aliasing={{0}: (2, {})} | custom-call | bytes 1048576 | tf_op jit(solution)/shard_map/level_gap/pallas_call | solution.py:630
  (1 shorter events, 0.0 us)
Async XLA Ops:
  3.2 13.1 %collective-permute-start.1 = (f32[512,128]{1,0:T(8,128)S(1)}, f32[512,128]{1,0:T(8,128)S(1)}, u32[]{:S(2)}, u32[]{:S(2)}) collective-permute-start(f32[512,128]{1,0:T(8,128)S(1)} %get-tuple-element.35), channel_id=1, source_target_pairs={{0,2},{2,0},{4,6},{6,4},{8,10},{10,8},{12,14},{14,12},{1,3},{3,1},... | collective-permute-start | bytes 786440 | tf_op jit(solution)/shard_map/ppermute | solution.py:556
  3.5 12.8 %collective-permute-start = (f32[512,128]{1,0:T(8,128)S(1)}, f32[512,128]{1,0:T(8,128)S(1)}, u32[]{:S(2)}, u32[]{:S(2)}) collective-permute-start(f32[512,128]{1,0:T(8,128)S(1)} %get-tuple-element.35), channel_id=1, source_target_pairs={{2,4},{6,8},{10,12},{4,2},{8,6},{12,10},{3,5},{7,9},{11,13},{5,3},... | collective-permute-start | bytes 786440 | tf_op jit(solution)/shard_map/ppermute | solution.py:557
  15.5 2.5 %collective-permute-start.2 = (f32[512,128]{1,0:T(8,128)S(1)}, f32[512,128]{1,0:T(8,128)S(1)}, u32[]{:S(2)}, u32[]{:S(2)}) collective-permute-start(f32[512,128]{1,0:T(8,128)S(1)} %get-tuple-element.41), channel_id=1, source_target_pairs={{0,16},{16,0},{1,17},{17,1},{2,18},{18,2},{3,19},{19,3},{4,20},{20... | collective-permute-start | bytes 786440 | tf_op jit(solution)/shard_map/ppermute | solution.py:579
  17.2 1.9 %collective-permute-start.3 = (f32[512,128]{1,0:T(8,128)S(1)}, f32[512,128]{1,0:T(8,128)S(1)}, u32[]{:S(2)}, u32[]{:S(2)}) collective-permute-start(f32[512,128]{1,0:T(8,128)S(1)} %get-tuple-element.47), channel_id=1, source_target_pairs={{0,16},{16,0},{1,17},{17,1},{2,18},{18,2},{3,19},{19,3},{4,20},{20... | collective-permute-start | bytes 786440 | tf_op jit(solution)/shard_map/ppermute | solution.py:608
